TPU v7x, 256 devices: a whole 4x4x8 slice. The times are simulated.
256 devices in a mesh: gx: 8 (over z_hi, core), gy: 8 (over y, z_lo), gz: 4 (over x).
Axes of the slice: x: 4, y: 4, z: 8 (z_hi: 4, z_lo: 2; z = z_hi * 2 + z_lo), core: 2. Of those that a mesh axis runs over, the one named last changes fastest.
Arguments:
- pressure_prev: float32 [128, 192, 1024], P('gx', 'gy', 'gz'), may hold values from -6 to 6
- pressure_now: float32 [128, 192, 1024], P('gx', 'gy', 'gz'), may hold values from -6 to 6
- material: int32 [128, 192, 1024], P('gx', 'gy', 'gz'), may hold values from 0 to 7
- speed_table: float32 [8], replicated, may hold values from 0.05 to 0.32
- anchors: int32 [8, 8, 512], P('gx', 'gy', 'gz'), may hold values from 0 to 53496, as said below
- counts: int32 [8, 8, 4], P('gx', 'gy', 'gz'), may hold values from 64 to 128, as said below
- w_in: bfloat16 [512, 1024], replicated, may hold values from -0.25 to 0.25
- w_out: bfloat16 [1024, 512], replicated, may hold values from -0.1875 to 0.1875
Outputs:
- final_pressure: float32 [128, 192, 1024], P('gx', 'gy', 'gz')
- grad_in: float32 [512, 1024], P('gx')
- grad_out: float32 [1024, 512], P('gx')
Inputs may be any that keep to these rules, and one draw needn't show every extreme that they name: `anchors`: each entry is i * 24 * 256 + j * 256 + k with i <= 8, j <= 16, k <= 248, so every patch lies inside its brick; entries of a brick may repeat. The used slots of a brick are its first counts slots.
All inputs are finite; a program needn't handle non-finite values.
Results may differ from a plain program's by a relative error of at most 0.0017.
Values sent between devices are 32-bit elements; how exact they have to be, the bound alone decides.
A program may use at most 64 MiB of HBM per device.

v0:
```python
import jax
import jax.numpy as jnp
from jax import lax
from jax.sharding import PartitionSpec as P

STEPS = 8
PATCH = 8


def extended(x, sides, width):
    for axis, dim in sides:
        peers, length = (lax.axis_size(axis), x.shape[dim])
        up = [(i, (i + 1) % peers) for i in range(peers - 1)]
        down = [(j, i) for i, j in up]
        last = lax.slice_in_dim(x, length - width, length, axis=dim)
        first = lax.slice_in_dim(x, 0, width, axis=dim)
        before = lax.ppermute(last, axis, up)
        after = lax.ppermute(first, axis, down)
        x = jnp.concatenate([before, x, after], axis=dim)
    return x


def coefficient(material, speed_table):
    coef = jnp.zeros(material.shape, jnp.float32)
    for number in range(speed_table.shape[0]):
        coef = jnp.where(material == number, speed_table[number], coef)
    return coef


def update(prev, now, coef, padded):
    beside = padded[2:, 1:-1, 1:-1] + padded[:-2, 1:-1, 1:-1]
    beside = beside + padded[1:-1, 2:, 1:-1] + padded[1:-1, :-2, 1:-1]
    beside = beside + padded[1:-1, 1:-1, 2:] + padded[1:-1, 1:-1, :-2]
    return 2.0 * now - prev + coef * (beside - 6.0 * now)


def outer_sum(left, right):
    return lax.dot_general(
        left, right, (((0,), (0,)), ((), ())), preferred_element_type=jnp.float32
    )


def mlp_parts(inputs, targets, valid, total, w_in, w_out):
    scale = lax.rsqrt(jnp.mean(inputs * inputs, axis=-1, keepdims=True) + 1e-06)
    normed = (inputs * scale).astype(jnp.bfloat16)
    pre = jnp.dot(normed, w_in, preferred_element_type=jnp.float32)
    act = jax.nn.gelu(pre).astype(jnp.bfloat16)
    err = inputs + jnp.dot(act, w_out, preferred_element_type=jnp.float32) - targets
    dout = (2.0 * err * valid[:, None] / total).astype(jnp.bfloat16)
    dact = lax.dot_general(
        dout, w_out, (((1,), (1,)), ((), ())), preferred_element_type=jnp.float32
    )
    dpre = jax.vjp(jax.nn.gelu, pre)[1](dact)[0].astype(jnp.bfloat16)
    return (normed, act, dout, dpre)


def body(pressure_prev, pressure_now, material, speed_table, anchors, counts, w_in, w_out):
    coef = coefficient(material, speed_table)
    cells_x, cells_y, cells_z = pressure_now.shape
    prev, now = (pressure_prev, pressure_now)
    for step in range(STEPS):
        padded = extended(now, (("gx", 0), ("gy", 1), ("gz", 2)), 1)
        prev, now = (now, update(prev, now, coef, padded))
    local = anchors.reshape(-1)
    edge = jnp.arange(PATCH, dtype=jnp.int32)
    offsets = (
        edge[:, None, None] * (cells_y * cells_z)
        + edge[None, :, None] * cells_z
        + edge[None, None, :]
    ).reshape(-1)
    cell_index = local[:, None] + offsets[None, :]
    inputs = jnp.take(pressure_now.reshape(-1), cell_index, axis=0)
    targets = jnp.take(now.reshape(-1), cell_index, axis=0)
    slots = local.shape[0]
    used = counts.reshape(())
    total = lax.psum(used.astype(jnp.float32), ("gx", "gy", "gz"))
    valid = (jnp.arange(slots, dtype=jnp.int32) < used).astype(jnp.float32)
    normed, act, dout, dpre = mlp_parts(inputs, targets, valid, total, w_in, w_out)
    groups = lax.axis_size("gx")
    in_count = normed.shape[1] // groups
    out_count = act.shape[1] // groups
    full_in = outer_sum(normed, dpre)
    full_out = outer_sum(act, dout)
    summed_in, summed_out = lax.psum((full_in, full_out), ("gx", "gy", "gz"))
    position = lax.axis_index("gx")
    grad_in = lax.dynamic_slice_in_dim(summed_in, position * in_count, in_count, 0)
    grad_out = lax.dynamic_slice_in_dim(summed_out, position * out_count, out_count, 0)
    return (now, grad_in, grad_out)


def solution(mesh):
    return jax.shard_map(
        body,
        mesh=mesh,
        in_specs=(
            P("gx", "gy", "gz"),
            P("gx", "gy", "gz"),
            P("gx", "gy", "gz"),
            P(),
            P("gx", "gy", "gz"),
            P("gx", "gy", "gz"),
            P(),
            P(),
        ),
        out_specs=(P("gx", "gy", "gz"), P("gx", None), P("gx", None)),
        check_vma=False,
    )
```

profile of v0, /device:TPU:8, one launch (start us, length us, event | category | flops | bytes accessed | tf_op | source)
XLA Modules:
  0.0 1375.7 jit_solution(7897120378503387624)
XLA Ops:
  12.3 3.8 collective-permute-done
  16.1 3.7 collective-permute-start.2
  22.0 4.4 collective-permute-done.3
  27.9 4.6 collective-permute-start.5
  33.2 4.1 collective-permute-done.4
  39.1 5.7 fusion.70
  46.1 3.4 collective-permute-start.7
  52.3 3.9 collective-permute-start.9
  56.2 2.6 collective-permute-done.9
  60.4 4.7 collective-permute-start.11
  65.1 5.0 collective-permute-done.10
  71.9 5.7 fusion.62
  78.9 3.3 collective-permute-start.13
  84.9 3.9 collective-permute-start.15
  88.9 2.7 collective-permute-done.15
  93.2 4.7 collective-permute-start.17
  97.8 2.7 collective-permute-done.16
  102.0 5.7 fusion.54
  109.0 6.3 collective-permute-start.19
  118.2 3.9 collective-permute-start.21
  122.1 2.6 collective-permute-done.21
  126.3 4.7 collective-permute-start.23
  131.0 2.7 collective-permute-done.22
  135.2 5.7 fusion.46
  142.2 7.6 collective-permute-start.25
  152.6 3.9 collective-permute-start.27
  156.5 2.6 collective-permute-done.27
  160.7 4.7 collective-permute-start.29
  165.4 2.7 collective-permute-done.28
  169.6 5.7 fusion.38
  176.6 7.6 collective-permute-start.31
  187.0 3.9 collective-permute-start.33
  191.0 2.6 collective-permute-done.33
  195.8 5.4 collective-permute-start.35
  204.7 6.6 fusion.30
  212.6 7.3 collective-permute-start.37
  223.4 3.9 collective-permute-start.39
  227.6 362.7 %gather_fusion = f32[65536]{0:T(1024)S(1)} fusion(f32[98304]{0:T(1024)S(1)} %bitcast.25, s32[65536]{0:T(1024)S(1)} %broadcast_clamp_fusion), kind=kCustom, calls=%fused_computation.clone | custom fusion | bytes 786432 | tf_op jit(solution)/shard_map/jit(_take)/gather | solution.py:72
  592.8 4.8 collective-permute-start.41
  601.9 6.5 fusion.22
  609.7 7.9 collective-permute-start.43
  618.5 3.1 collective-permute-start.44
  621.6 3.0 collective-permute-start.45
  630.4 5.4 collective-permute-start.47
  635.9 83.4 %psum.21 = f32[]{:T(128)} all-reduce(f32[]{:T(128)S(6)} %convert_element_type.22), channel_id=1, replica_groups=mesh['gx'=8,'gy'=8,'gz'=4] {'gx','gy','gz'}, use_global_device_ids=true, to_apply=%region_1.3 | all-reduce | flops 1 | bytes 8 | tf_op jit(solution)/shard_map/psum | solution.py:76
  719.9 6.7 fusion.14
  726.8 362.7 %gather_fusion.1 = f32[65536]{0:T(1024)S(1)} fusion(f32[98304]{0:T(1024)S(1)} %bitcast.24, s32[65536]{0:T(1024)S(1)} %broadcast_clamp_fusion), kind=kCustom, calls=%fused_computation.1.clone | custom fusion | bytes 786432 | tf_op jit(solution)/shard_map/jit(_take)/gather | solution.py:73
  1095.0 270.5 %all-reduce.3.cloned.1.call-done = (f32[512,1024]{1,0:T(8,128)}, f32[1024,512]{1,0:T(8,128)}) async-done(((f32[512,1024]{1,0:T(8,128)}, f32[1024,512]{1,0:T(8,128)}), (f32[512,1024]{1,0:T(8,128)}, f32[1024,512]{1,0:T(8,128)})) %all-reduce.3.cloned.1.call-update) | async-done | bytes 4194320 | tf_op jit(solution)/shard_map/psum | solution.py:84
  (146 shorter events, 78.0 us)
Async XLA Ops:
  7.2 1358.3 %all-reduce.3.cloned.1.call-start = ((), (), s32[]{:S(2)}) async-start(), calls=%async_computation | async-start | bytes 8388608 | tf_op jit(solution)/shard_map/psum | solution.py:84
  9.9 6.1 collective-permute-start
  16.1 5.9 collective-permute-start.2
  19.8 6.6 collective-permute-start.3
  26.6 10.7 collective-permute-start.4
  27.9 11.2 collective-permute-start.5
  44.8 4.7 collective-permute-start.6
  46.1 4.3 collective-permute-start.7
  50.4 5.9 collective-permute-start.8
  52.3 6.6 collective-permute-start.9
  59.1 11.1 collective-permute-start.10
  60.4 11.5 collective-permute-start.11
  77.6 4.6 collective-permute-start.12
  78.9 4.1 collective-permute-start.13
  83.0 5.9 collective-permute-start.14
  84.9 6.7 collective-permute-start.15
  91.9 8.7 collective-permute-start.16
  93.2 8.9 collective-permute-start.17
  107.7 7.6 collective-permute-start.18
  109.0 7.2 collective-permute-start.19
  116.2 5.9 collective-permute-start.20
  118.2 6.6 collective-permute-start.21
  125.0 8.8 collective-permute-start.22
  126.3 8.9 collective-permute-start.23
  140.9 8.9 collective-permute-start.24
  142.2 8.4 collective-permute-start.25
  150.6 5.9 collective-permute-start.26
  152.6 6.6 collective-permute-start.27
  159.4 8.8 collective-permute-start.28
  160.7 8.9 collective-permute-start.29
  175.3 8.9 collective-permute-start.30
  176.6 8.4 collective-permute-start.31
  185.1 5.9 collective-permute-start.32
  187.0 6.6 collective-permute-start.33
  194.5 9.0 collective-permute-start.34
  195.8 9.0 collective-permute-start.35
  211.3 8.8 collective-permute-start.36
  212.6 8.2 collective-permute-start.37
  221.4 368.9 %collective-permute-start.38 = (f32[18,1,256]{2,1,0:T(1,128)}, f32[18,1,256]{2,1,0:T(1,128)}, u32[]{:S(2)}, u32[]{:S(2)}) collective-permute-start(f32[18,1,256]{2,1,0:T(1,128)} %get-tuple-element.25), channel_id=1, source_target_pairs={{4,0},{8,4},{12,8},{16,12},{20,16},{24,20},{28,24},{5,1},{9,5},{13... | collective-permute-start | bytes 55304 | tf_op jit(solution)/shard_map/ppermute | solution.py:18
  223.4 367.0 %collective-permute-start.39 = (f32[18,1,256]{2,1,0:T(1,128)}, f32[18,1,256]{2,1,0:T(1,128)}, u32[]{:S(2)}, u32[]{:S(2)}) collective-permute-start(f32[18,1,256]{2,1,0:T(1,128)} %get-tuple-element.24), channel_id=1, source_target_pairs={{0,4},{4,8},{8,12},{12,16},{16,20},{20,24},{24,28},{1,5},{5,9},{9,... | collective-permute-start | bytes 55304 | tf_op jit(solution)/shard_map/ppermute | solution.py:17
  591.4 9.0 collective-permute-start.40
  592.8 9.1 collective-permute-start.41
  608.4 9.3 collective-permute-start.42
  609.7 8.8 collective-permute-start.43
  618.5 8.0 collective-permute-start.44
  621.6 6.6 collective-permute-start.45
  629.1 90.1 %collective-permute-start.46 = (f32[18,26,1]{2,1,0:T(8,128)}, f32[18,26,1]{2,1,0:T(8,128)S(1)}, u32[]{:S(2)}, u32[]{:S(2)}) collective-permute-start(f32[18,26,1]{2,1,0:T(8,128)} %get-tuple-element.6), channel_id=1, source_target_pairs={{1,0},{2,1},{3,2},{5,4},{6,5},{7,6},{9,8},{10,9},{11,10},{13,12},{... | collective-permute-start | bytes 5624 | tf_op jit(solution)/shard_map/ppermute | solution.py:18
  630.4 89.5 %collective-permute-start.47 = (f32[18,26,1]{2,1,0:T(8,128)}, f32[18,26,1]{2,1,0:T(8,128)}, u32[]{:S(2)}, u32[]{:S(2)}) collective-permute-start(f32[18,26,1]{2,1,0:T(8,128)} %get-tuple-element.7), channel_id=1, source_target_pairs={{0,1},{1,2},{2,3},{4,5},{5,6},{6,7},{8,9},{9,10},{10,11},{12,13},{... | collective-permute-start | bytes 5624 | tf_op jit(solution)/shard_map/ppermute | solution.py:17
  (15 other events, 2734.5 us)
Sparse Core Ops, SparseCore 0:
  1095.1 270.3 all-reduce.2
where the time goes:
time: 1380 us
  local copies, waits for them, and re-layouts  735 us (53%)
  waiting for transfers between devices  332 us (24%)
  starting transfers between devices  152 us (11%)
  blocking collectives  83.4 us (6%)
  other arithmetic  50.9 us (4%)
  between operations  15.7 us (1%)
    gather x2, local copies, waits for them, and re-layouts, body(): inputs = jnp.take(pressure_now.reshape(-1), cell_index, axis=0)  363 us
    gather x2, local copies, waits for them, and re-layouts, body(): targets = jnp.take(now.reshape(-1), cell_index, axis=0)  363 us
    psum x1, waiting for transfers between devices, body(): summed_in, summed_out = lax.psum((full_in, full_out), ('gx', 'gy', 'gz'))  271 us
    ppermute x24, starting transfers between devices, extended(): before = lax.ppermute(last, axis, up)  113 us
    psum x1, blocking collectives, body(): total = lax.psum(used.astype(jnp.float32), ('gx', 'gy', 'gz'))  83.4 us
    add x8, other arithmetic, update(): return 2.0 * now - prev + coef * (beside - 6.0 * now)  48.1 us
    ppermute x24, starting transfers between devices, extended(): after = lax.ppermute(first, axis, down)  39.2 us
    ppermute x24, waiting for transfers between devices, extended(): before = lax.ppermute(last, axis, up)  35.3 us
  transfers between devices with their start and end apart: 49, of which 30 were waited for; matrix products, arithmetic and copies ran while one was open for 27% of the time, Pallas kernels for 0%

commit v1 on v0

v1 whole, which is shorter than its diff:
```python
import functools

import jax
import jax.numpy as jnp
from jax import lax
from jax.experimental import pallas as pl
from jax.experimental.pallas import tpu as pltpu
from jax.sharding import PartitionSpec as P

STEPS = 8
PATCH = 8
LANES = 128
AXES = ("gx", "gy", "gz")
F32 = jnp.float32
BF16 = jnp.bfloat16


def remote(src, dst, send_sem, recv_sem, device):
    return pltpu.make_async_remote_copy(
        src_ref=src,
        dst_ref=dst,
        send_sem=send_sem,
        recv_sem=recv_sem,
        device_id=device,
        device_id_type=pl.DeviceIdType.MESH,
    )


def signal(sem, device):
    pl.semaphore_signal(
        sem, inc=1, device_id=device, device_id_type=pl.DeviceIdType.MESH
    )


def wave_kernel(
    sizes,
    prev_ref,
    now_ref,
    mat_ref,
    tab_ref,
    cnt_ref,
    out_ref,
    tot_ref,
    buf_a,
    buf_b,
    coef,
    ysend,
    yrecv,
    zsend,
    zrecv,
    csend,
    crecv,
    xs,
    xr,
    ys,
    yr,
    zs,
    zr,
    cs,
    cr,
):
    nx, ny, nz = sizes
    gx, gy, gz = [lax.axis_index(axis) for axis in AXES]
    X, Y, Z = now_ref.shape
    W = Z + LANES
    here = (gx, gy, gz)

    def line_peer(axis, step):
        size = sizes[axis]
        device = list(here)
        device[axis] = lax.rem(here[axis] + step, size)
        return tuple(device)

    zero_plane = jnp.zeros((Y, W), F32)
    for buf in (buf_a, buf_b):
        buf[0] = zero_plane
        buf[X + 1] = zero_plane
    yrecv[...] = jnp.zeros(yrecv.shape, F32)
    zrecv[...] = jnp.zeros(zrecv.shape, F32)

    barrier = pltpu.get_barrier_semaphore()
    peers = 0
    for axis in range(3):
        for step in range(1, sizes[axis]):
            signal(barrier, line_peer(axis, step))
            peers += 1

    lane = lax.broadcasted_iota(jnp.int32, (Y, LANES), 1)
    row = lax.broadcasted_iota(jnp.int32, (Y, W), 0)

    def pack(x, carry):
        material = mat_ref[x]
        c = jnp.zeros((Y, Z), F32)
        for number in range(tab_ref.shape[0]):
            c = jnp.where(material == number, tab_ref[number], c)
        n, p = now_ref[x], prev_ref[x]
        coef[x, :, 0:Z] = c
        buf_a[x + 1, :, 0:Z] = n
        buf_b[x + 1, :, 0:Z] = p
        mine = lax.shift_right_logical(lane, 3) == x
        up, down = [], []
        for field, held_up, held_down in zip((n, p, c), carry[0], carry[1]):
            last = pltpu.roll(field[:, Z - LANES :], lax.rem(x * 8 + 8, LANES), 1)
            first = pltpu.roll(field[:, :LANES], x * 8, 1)
            up.append(jnp.where(mine, last, held_up))
            down.append(jnp.where(mine, first, held_down))
        return tuple(up), tuple(down)

    empty = tuple(jnp.zeros((Y, LANES), F32) for _ in range(3))
    ups, downs = lax.fori_loop(0, X, pack, (empty, empty))
    for i in range(3):
        zsend[0, i] = ups[i]
        zsend[1, i] = downs[i]
    csend[0] = jnp.full((8, LANES), cnt_ref[0].astype(F32))

    pl.semaphore_wait(barrier, peers)

    def z_up():
        return remote(
            zsend.at[0], zrecv.at[0], zs.at[0], zr.at[0], (gx, gy, lax.rem(gz + 1, nz))
        )

    def z_down():
        return remote(
            zsend.at[1],
            zrecv.at[1],
            zs.at[1],
            zr.at[1],
            (gx, gy, lax.rem(gz + nz - 1, nz)),
        )

    @pl.when(gz < nz - 1)
    def _():
        z_up().start()

    @pl.when(gz > 0)
    def _():
        z_down().start()

    def count_copy(axis, step):
        return remote(
            csend.at[axis],
            crecv.at[axis, here[axis]],
            cs.at[axis, step],
            cr.at[axis, here[axis]],
            line_peer(axis, step),
        )

    def count_start(axis):
        for step in range(1, sizes[axis]):
            count_copy(axis, step).start()
        crecv[axis, here[axis]] = csend[axis]

    def count_finish(axis):
        size = sizes[axis]
        for step in range(1, size):
            count_copy(axis, step).wait_send()
            source = lax.rem(here[axis] + step, size)
            remote(
                csend.at[axis],
                crecv.at[axis, source],
                cs.at[axis, step],
                cr.at[axis, source],
                line_peer(axis, step),
            ).wait_recv()
        total = crecv[axis, 0]
        for i in range(1, size):
            total = total + crecv[axis, i]
        return total

    count_start(0)

    @pl.when(gz < nz - 1)
    def _():
        z_up().wait_send()
        z_down().wait_recv()

    @pl.when(gz > 0)
    def _():
        z_down().wait_send()
        z_up().wait_recv()

    def unpack(x, carry):
        outer = []
        for i in range(3):
            left = pltpu.roll(zrecv[0, i], lax.rem(120 + LANES - x * 8, LANES), 1)
            right = pltpu.roll(zrecv[1, i], lax.rem(LANES - x * 8, LANES), 1)
            outer.append(
                jnp.where(lane < 8, right, jnp.where(lane >= 120, left, 0.0))
            )
        buf_a[x + 1, :, Z:W] = outer[0]
        buf_b[x + 1, :, Z:W] = outer[1]
        coef[x, :, Z:W] = outer[2]
        ysend[0, 0, x, :, 0:Z] = now_ref[x, 0:1, :]
        ysend[0, 0, x, :, Z:W] = outer[0][0:1]
        ysend[0, 1, x, :, 0:Z] = now_ref[x, Y - 1 : Y, :]
        ysend[0, 1, x, :, Z:W] = outer[0][Y - 1 : Y]
        return carry

    lax.fori_loop(0, X, unpack, 0)

    bufs = (buf_a, buf_b)

    def face(which, par):
        buf = bufs[par]
        if which == 0:
            return remote(
                buf.at[1],
                buf.at[X + 1],
                xs.at[par, 0],
                xr.at[par, 1],
                (lax.rem(gx + nx - 1, nx), gy, gz),
            )
        if which == 1:
            return remote(
                buf.at[X],
                buf.at[0],
                xs.at[par, 1],
                xr.at[par, 0],
                (lax.rem(gx + 1, nx), gy, gz),
            )
        if which == 2:
            return remote(
                ysend.at[par, 0],
                yrecv.at[par, 1],
                ys.at[par, 0],
                yr.at[par, 1],
                (gx, lax.rem(gy + ny - 1, ny), gz),
            )
        return remote(
            ysend.at[par, 1],
            yrecv.at[par, 0],
            ys.at[par, 1],
            yr.at[par, 0],
            (gx, lax.rem(gy + 1, ny), gz),
        )

    has = (gx > 0, gx < nx - 1, gy > 0, gy < ny - 1)
    opposite = (1, 0, 3, 2)

    def faces_start(par):
        for which in range(4):

            @pl.when(has[which])
            def _():
                face(which, par).start()

    def faces_sent(par):
        for which in range(4):

            @pl.when(has[which])
            def _():
                face(which, par).wait_send()

    def faces_here(par):
        for which in range(4):

            @pl.when(has[which])
            def _():
                face(opposite[which], par).wait_recv()

    faces_start(0)
    for t in range(STEPS):
        par = t % 2
        cur, other = bufs[par], bufs[1 - par]
        faces_here(par)
        if t > 0:
            faces_sent(1 - par)
        last_step = t == STEPS - 1

        def plane(x, carry):
            n = cur[x + 1]
            beside = cur[x + 2] + cur[x]
            low = yrecv[par, 0, x]
            high = yrecv[par, 1, x]
            beside = beside + jnp.where(row == Y - 1, high, pltpu.roll(n, Y - 1, 0))
            beside = beside + jnp.where(row == 0, low, pltpu.roll(n, 1, 0))
            beside = beside + pltpu.roll(n, W - 1, 1) + pltpu.roll(n, 1, 1)
            after = 2.0 * n - other[x + 1] + coef[x] * (beside - 6.0 * n)
            if last_step:
                out_ref[x] = after[:, 0:Z]
            else:
                other[x + 1] = after
                ysend[1 - par, 0, x] = after[0:1]
                ysend[1 - par, 1, x] = after[Y - 1 : Y]
            return carry

        lax.fori_loop(0, X, plane, 0)
        if not last_step:
            faces_start(1 - par)
        if t == 1:
            csend[1] = count_finish(0)
            count_start(1)
        if t == 3:
            csend[2] = count_finish(1)
            count_start(2)
        if t == 5:
            tot_ref[...] = count_finish(2)
    faces_sent(1)


def wave(prev, now, material, table, used, sizes):
    X, Y, Z = now.shape
    W = Z + LANES
    vmem = pl.BlockSpec(memory_space=pltpu.VMEM)
    smem = pl.BlockSpec(memory_space=pltpu.SMEM)
    dma = pltpu.SemaphoreType.DMA
    most = max(sizes)
    return pl.pallas_call(
        functools.partial(wave_kernel, sizes),
        name="wave",
        out_shape=(
            jax.ShapeDtypeStruct((X, Y, Z), F32),
            jax.ShapeDtypeStruct((8, LANES), F32),
        ),
        in_specs=[vmem, vmem, vmem, smem, smem],
        out_specs=(vmem, vmem),
        scratch_shapes=[
            pltpu.VMEM((X + 2, Y, W), F32),
            pltpu.VMEM((X + 2, Y, W), F32),
            pltpu.VMEM((X, Y, W), F32),
            pltpu.VMEM((2, 2, X, 1, W), F32),
            pltpu.VMEM((2, 2, X, 1, W), F32),
            pltpu.VMEM((2, 3, Y, LANES), F32),
            pltpu.VMEM((2, 3, Y, LANES), F32),
            pltpu.VMEM((3, 8, LANES), F32),
            pltpu.VMEM((3, most, 8, LANES), F32),
            dma((2, 2)),
            dma((2, 2)),
            dma((2, 2)),
            dma((2, 2)),
            dma((2,)),
            dma((2,)),
            dma((3, most)),
            dma((3, most)),
        ],
        compiler_params=pltpu.CompilerParams(collective_id=0, has_side_effects=True),
    )(prev, now, material, table, used)


def matmul(a, b, dims):
    return lax.dot_general(a, b, (dims, ((), ())), preferred_element_type=F32)


def in_order(values, order):
    total = None
    rest = values
    for part in range(3):
        piece = rest.astype(BF16)
        if part < 2:
            rest = rest - piece.astype(F32)
        term = matmul(piece, order, ((1,), (0,)))
        total = term if total is None else total + term
    return total


def patch_kernel(
    blocks,
    now_ref,
    final_ref,
    anchor_ref,
    cnt_ref,
    tot_ref,
    win_ref,
    wout_ref,
    grad_ref,
    rows,
    turned,
    picked,
    order,
):
    X, Y, Z = now_ref.shape
    slots = anchor_ref.shape[0]
    wide = win_ref.shape[0]
    hidden = win_ref.shape[1]
    tiles = X * Y // LANES

    for which, field in enumerate((now_ref, final_ref)):
        for x in range(X):
            for half in range(Z // LANES):
                rows[half, pl.ds(x, Y, stride=X), :] = field[
                    x, :, half * LANES : (half + 1) * LANES
                ]
        for half in range(Z // LANES):
            for tile in range(tiles):
                turned[which, tile, half * LANES : (half + 1) * LANES, :] = rows[
                    half, tile * LANES : (tile + 1) * LANES, :
                ].T
        turned[which, tiles] = jnp.zeros((Z, LANES), F32)

    lane = lax.broadcasted_iota(jnp.int32, (8, LANES), 1)

    def pick(s, carry):
        anchor = anchor_ref[s]
        i = anchor // (Y * Z)
        j = lax.rem(anchor // Z, Y)
        k = lax.rem(anchor, Z)
        shift = j * X + i
        tile = shift // LANES
        by = lax.rem(shift, LANES)
        back = lax.rem(LANES - by, LANES)
        for which in range(2):
            first = turned[which, tile, pl.ds(k, 8), :]
            second = turned[which, tile + 1, pl.ds(k, 8), :]
            value = jnp.where(
                lane < LANES - by,
                pltpu.roll(first, back, 1),
                pltpu.roll(second, back, 1),
            )
            picked[which, pl.ds(pl.multiple_of(s * 8, 8), 8), :] = value
        return carry

    lax.fori_loop(0, slots, pick, 0, unroll=4)

    at = lax.broadcasted_iota(jnp.int32, (8 * LANES, wide), 0)
    feature = lax.broadcasted_iota(jnp.int32, (8 * LANES, wide), 1)
    a = jnp.bitwise_and(at, X - 1)
    b = jnp.bitwise_and(lax.shift_right_logical(at, 4), 7)
    c = lax.shift_right_logical(at, 7)
    order[...] = jnp.where(
        (a < PATCH) & (feature == a * 64 + b * 8 + c), 1.0, 0.0
    ).astype(BF16)

    taken = []
    for which in range(2):
        values = jnp.concatenate(
            [picked[which, pl.ds(c, slots, stride=8), :] for c in range(8)], axis=1
        )
        taken.append(in_order(values, order[...]))
    inputs, targets = taken

    mean = jnp.mean(inputs * inputs, axis=1, keepdims=True)
    normed = (inputs * lax.rsqrt(mean + 1e-06)).astype(BF16)
    pre = matmul(normed, win_ref[...], ((1,), (0,)))
    root = 0.7978845608028654
    tanh = jnp.tanh(root * (pre + 0.044715 * (pre * pre * pre)))
    cdf = 0.5 * (1.0 + tanh)
    act = (pre * cdf).astype(BF16)
    slope = cdf + 0.5 * pre * (1.0 - tanh * tanh) * (
        root * (1.0 + (3.0 * 0.044715) * (pre * pre))
    )
    err = inputs + matmul(act, wout_ref[...], ((1,), (0,))) - targets
    slot = lax.broadcasted_iota(jnp.int32, (slots, 1), 0)
    valid = (slot < cnt_ref[0]).astype(F32)
    dout = (2.0 * err * valid / tot_ref[0:1, 0:1]).astype(BF16)
    dact = matmul(dout, wout_ref[...], ((1,), (1,)))
    dpre = (dact * slope).astype(BF16)
    grad_in = matmul(normed, dpre, ((0,), (0,)))
    grad_out = matmul(act, dout, ((0,), (0,)))
    in_rows = wide // blocks
    out_rows = hidden // blocks
    for block in range(blocks):
        core, high = block % 2, block // 2
        grad_ref[core, high, 0:in_rows, :] = grad_in[
            block * in_rows : (block + 1) * in_rows
        ]
        for half in range(2):
            start = block * out_rows + half * in_rows
            grad_ref[
                core, high, in_rows : 2 * in_rows, half * wide : (half + 1) * wide
            ] = grad_out[start : start + in_rows]


def patches(now, final, anchors, used, total, w_in, w_out, blocks):
    X, Y, Z = now.shape
    slots = anchors.shape[0]
    wide, hidden = w_in.shape
    vmem = pl.BlockSpec(memory_space=pltpu.VMEM)
    smem = pl.BlockSpec(memory_space=pltpu.SMEM)
    return pl.pallas_call(
        functools.partial(patch_kernel, blocks),
        name="patches",
        out_shape=jax.ShapeDtypeStruct(
            (2, blocks // 2, 2 * wide // blocks, hidden), F32
        ),
        in_specs=[vmem, vmem, smem, smem, vmem, vmem, vmem],
        out_specs=vmem,
        scratch_shapes=[
            pltpu.VMEM((Z // LANES, X * Y, LANES), F32),
            pltpu.VMEM((2, X * Y // LANES + 1, Z, LANES), F32),
            pltpu.VMEM((2, 8 * slots, LANES), F32),
            pltpu.VMEM((8 * LANES, wide), BF16),
        ],
        compiler_params=pltpu.CompilerParams(vmem_limit_bytes=60 * 1024 * 1024),
    )(now, final, anchors, used, total, w_in, w_out)


def reduce_kernel(
    grad_ref,
    in_ref,
    out_ref,
    pair,
    relay1,
    fin1,
    send1,
    held1,
    relay2,
    fin2,
    send2,
    held2,
    zrecv,
    gathered,
    pair_sem,
    sems1,
    sems2,
    z_send,
    z_recv,
    g_send,
    g_recv,
):
    gx, gy, gz = [lax.axis_index(axis) for axis in AXES]
    core, high = lax.rem(gx, 2), gx // 2
    low, y = lax.rem(gy, 2), gy // 2
    x = gz

    def device(core=core, high=high, low=low, y=y, x=x):
        return (high * 2 + core, y * 2 + low, x)

    barrier = pltpu.get_barrier_semaphore()
    signal(barrier, device(core=1 - core))
    peers = 1
    z_steps = [(h, l) for h in range(4) for l in range(2) if h or l]
    g_steps = [
        (i, j, l) for i in range(4) for j in range(4) for l in range(2) if i or j or l
    ]
    for h, l in z_steps:
        if h:
            signal(
                barrier, device(high=lax.rem(high + h, 4), low=lax.rem(low + l, 2))
            )
            peers += 1
    for i, j, l in g_steps:
        signal(
            barrier,
            device(x=lax.rem(x + i, 4), y=lax.rem(y + j, 4), low=lax.rem(low + l, 2)),
        )
        peers += 1
    pl.semaphore_wait(barrier, peers)

    swap = remote(
        grad_ref.at[1 - core],
        pair,
        pair_sem.at[0],
        pair_sem.at[1],
        device(core=1 - core),
    )
    swap.start()
    swap.wait()
    for h in range(4):
        pair[h] = pair[h] + grad_ref[core, h]

    half = 512
    places = ((x, lambda v: device(x=v)), (y, lambda v: device(y=v)))

    def ring(stage, colour, source, rows, relay, fin, send, sems):
        along = colour if stage == 0 else 1 - colour
        me, to = places[along]
        plus, minus, across = [lax.rem(me + d, 4) for d in (1, 3, 2)]

        def chunk(owner):
            return pl.ds(pl.multiple_of(owner * rows, 8), rows)

        first, second = pl.ds(0, 2), pl.ds(2, 2)

        def piece(part, owner):
            return source(part, chunk(owner))

        def copy(src, dst, number, peer):
            return remote(
                src,
                dst,
                sems.at[colour, 0, number],
                sems.at[colour, 1, number],
                to(peer),
            )

        copies = [
            copy(piece(first, across), relay.at[colour, 0], 0, plus),
            copy(piece(second, across), relay.at[colour, 1], 1, minus),
            copy(piece(second, plus), fin.at[colour, 0, second], 2, plus),
            copy(piece(first, minus), fin.at[colour, 1, first], 3, minus),
            copy(send.at[colour, 0], fin.at[colour, 0, first], 4, plus),
            copy(send.at[colour, 1], fin.at[colour, 1, second], 5, minus),
        ]

        def start():
            for one in copies[:4]:
                one.start()

        def forward():
            copies[0].wait_recv()
            send[colour, 0] = relay[colour, 0] + piece(first, plus)[...]
            copies[4].start()
            copies[1].wait_recv()
            send[colour, 1] = relay[colour, 1] + piece(second, minus)[...]
            copies[5].start()

        def finish():
            for one in copies[2:]:
                one.wait_recv()
            own = piece(pl.ds(0, 4), me)[...]
            total = own + fin[colour, 0] + fin[colour, 1]
            for one in copies:
                one.wait_send()
            return total

        return start, forward, finish

    def source1(colour):
        def pick(part, rows):
            return pair.at[part, rows, pl.ds(colour * half, half)]

        return pick

    def source2(colour):
        def pick(part, rows):
            return held1.at[colour, part, rows, :]

        return pick

    stage1 = [
        ring(0, colour, source1(colour), 32, relay1, fin1, send1, sems1)
        for colour in range(2)
    ]
    stage2 = [
        ring(1, colour, source2(colour), 8, relay2, fin2, send2, sems2)
        for colour in range(2)
    ]
    for rings, held in ((stage1, held1), (stage2, held2)):
        for one in rings:
            one[0]()
        for one in rings:
            one[1]()
        for colour, one in enumerate(rings):
            held[colour] = one[2]()

    z_me = high * 2 + low
    quarter = half // 2

    def z_piece(h, l):
        return held2.at[:, h, :, pl.ds(pl.multiple_of(l * quarter, quarter), quarter)]

    z_copies = []
    for number, (h, l) in enumerate(z_steps):
        ph, pw = lax.rem(high + h, 4), lax.rem(low + l, 2)
        one = remote(
            z_piece(ph, pw),
            zrecv.at[z_me],
            z_send.at[number],
            z_recv.at[z_me],
            device(high=ph, low=pw),
        )
        one.start()
        z_copies.append((one, ph * 2 + pw, device(high=ph, low=pw)))
    zrecv[z_me] = z_piece(high, low)[...]
    for one, slot, peer in z_copies:
        remote(
            z_piece(high, low), zrecv.at[slot], z_send.at[0], z_recv.at[slot], peer
        ).wait_recv()
    total = zrecv[0]
    for slot in range(1, 8):
        total = total + zrecv[slot]
    g_me = (x * 4 + y) * 2 + low
    gathered[g_me] = total
    g_copies = []
    for number, (i, j, l) in enumerate(g_steps):
        px, py, pw = lax.rem(x + i, 4), lax.rem(y + j, 4), lax.rem(low + l, 2)
        peer = device(x=px, y=py, low=pw)
        one = remote(
            gathered.at[g_me],
            gathered.at[g_me],
            g_send.at[number],
            g_recv.at[g_me],
            peer,
        )
        one.start()
        g_copies.append((one, (px * 4 + py) * 2 + pw, peer))
    for one, slot, peer in z_copies:
        one.wait_send()
    for one, slot, peer in g_copies:
        remote(
            gathered.at[slot],
            gathered.at[slot],
            g_send.at[0],
            g_recv.at[slot],
            peer,
        ).wait_recv()
    for ix in range(4):
        for iy in range(4):
            for il in range(2):
                slot = (ix * 4 + iy) * 2 + il
                for colour in range(2):
                    row = ix * 32 + iy * 8 if colour == 0 else iy * 32 + ix * 8
                    at = colour * half + il * quarter
                    value = gathered[slot, colour]
                    if row < 64:
                        in_ref[row : row + 8, at : at + quarter] = value
                    else:
                        top = row - 64 + (64 if at >= 512 else 0)
                        left = at % 512
                        out_ref[top : top + 8, left : left + quarter] = value
    for one, slot, peer in g_copies:
        one.wait_send()


def reduce(grads):
    vmem = pl.BlockSpec(memory_space=pltpu.VMEM)
    dma = pltpu.SemaphoreType.DMA
    return pl.pallas_call(
        reduce_kernel,
        name="reduce",
        out_shape=(
            jax.ShapeDtypeStruct((64, 1024), F32),
            jax.ShapeDtypeStruct((128, 512), F32),
        ),
        in_specs=[vmem],
        out_specs=(vmem, vmem),
        scratch_shapes=[
            pltpu.VMEM((4, 128, 1024), F32),
            pltpu.VMEM((2, 2, 2, 32, 512), F32),
            pltpu.VMEM((2, 2, 4, 32, 512), F32),
            pltpu.VMEM((2, 2, 2, 32, 512), F32),
            pltpu.VMEM((2, 4, 32, 512), F32),
            pltpu.VMEM((2, 2, 2, 8, 512), F32),
            pltpu.VMEM((2, 2, 4, 8, 512), F32),
            pltpu.VMEM((2, 2, 2, 8, 512), F32),
            pltpu.VMEM((2, 4, 8, 512), F32),
            pltpu.VMEM((8, 2, 8, 256), F32),
            pltpu.VMEM((32, 2, 8, 256), F32),
            dma((2,)),
            dma((2, 2, 6)),
            dma((2, 2, 6)),
            dma((7,)),
            dma((8,)),
            dma((31,)),
            dma((32,)),
        ],
        compiler_params=pltpu.CompilerParams(
            collective_id=1,
            has_side_effects=True,
            vmem_limit_bytes=60 * 1024 * 1024,
        ),
    )(grads)


def body(pressure_prev, pressure_now, material, speed_table, anchors, counts, w_in, w_out):
    sizes = tuple(lax.axis_size(axis) for axis in AXES)
    used = counts.reshape(-1)
    final, total = wave(
        pressure_prev, pressure_now, material, speed_table, used, sizes
    )
    grads = patches(
        pressure_now, final, anchors.reshape(-1), used, total, w_in, w_out, sizes[0]
    )
    grad_in, grad_out = reduce(grads)
    return final, grad_in, grad_out


def solution(mesh):
    return jax.shard_map(
        body,
        mesh=mesh,
        in_specs=(
            P("gx", "gy", "gz"),
            P("gx", "gy", "gz"),
            P("gx", "gy", "gz"),
            P(),
            P("gx", "gy", "gz"),
            P("gx", "gy", "gz"),
            P(),
            P(),
        ),
        out_specs=(P("gx", "gy", "gz"), P("gx", None), P("gx", None)),
        check_vma=False,
    )
```

time: 1380 us -> 118 us (0.09)
  local copies, waits for them, and re-layouts: 735 us -> 4.09 us
  waiting for transfers between devices: 332 us -> 0 us
  starting transfers between devices: 152 us -> 0 us
  Pallas kernels: 0 us -> 112 us
  blocking collectives: 83.4 us -> 0 us
  other arithmetic: 50.9 us -> 0 us
  between operations: 15.7 us -> 1.31 us
    gather x4 -> x0, local copies, waits for them, and re-layouts: 725 us -> none  [the longest x2 363 us: body(): inputs = jnp.take(pressure_now.reshape(-1), cell_index, axis=0)]
    psum x1 -> x0, waiting for transfers between devices: 271 us -> none  [body(): summed_in, summed_out = lax.psum((full_in, full_out), ('gx', 'gy', 'gz'))]
    ppermute x48 -> x0, starting transfers between devices: 152 us -> none  [the longest x24 113 us: extended(): before = lax.ppermute(last, axis, up)]
    pallas_call x0 -> x3, Pallas kernels: none -> 112 us  [the longest x1 55.4 us: wave(): pl.pallas_call(functools.partial(wave_kernel, sizes), name='wave', out_sh...]
    psum x1 -> x0, blocking collectives: 83.4 us -> none  [body(): total = lax.psum(used.astype(jnp.float32), ('gx', 'gy', 'gz'))]
    ppermute x48 -> x0, waiting for transfers between devices: 61.1 us -> none  [the longest x24 35.3 us: extended(): before = lax.ppermute(last, axis, up)]
    add x10 -> x0, other arithmetic: 48.2 us -> none  [the longest x8 48.1 us: update(): return 2.0 * now - prev + coef * (beside - 6.0 * now)]
  transfers between devices with their start and end apart: 49 -> 0, of which waited for: 30 -> 0; matrix products, arithmetic and copies ran while one was open for 27% -> 0% of each run, Pallas kernels for 0% -> 0%
where the time goes in v1:
time: 118 us; the launch traced here: 117 us
  Pallas kernels  112 us (95%)
  local copies, waits for them, and re-layouts  4.09 us (3%)
  between operations  1.31 us (1%)
    pallas_call x1, Pallas kernels, wave(): pl.pallas_call(functools.partial(wave_kernel, sizes), name='wave', out_sh...  55.4 us
    pallas_call x1, Pallas kernels, reduce(): pl.pallas_call(reduce_kernel, name='reduce', out_shape=(jax.ShapeDtypeStr...  46 us
    pallas_call x1, Pallas kernels, patches(): pl.pallas_call(functools.partial(patch_kernel, blocks), name='patches', o...  10.4 us
    unnamed x5, local copies, waits for them, and re-layouts  4.09 us

profile of v1, /device:TPU:8, one launch (start us, length us, event | category | flops | bytes accessed | tf_op | source)
XLA Modules:
  0.0 117.2 jit_solution(11277403521868593668)
XLA Ops:
  1.3 55.4 %wave.1 = (f32[16,24,256]{2,1,0:T(8,128)}, f32[8,128]{1,0:T(8,128)}) custom-call(f32[16,24,256]{2,1,0:T(8,128)} %prev_ref.1, f32[16,24,256]{2,1,0:T(8,128)} %now_ref.3, s32[16,24,256]{2,1,0:T(8,128)} %mat_ref.1, f32[8]{0:T(128)} %tab_ref.1, s32[1]{0:T(128)} %bitcast.2.cnt_ref), custom_call_target="tpu_custom_call" | custom-call | tf_op jit(solution)/shard_map/wave/pallas_call | solution.py:309
  56.7 0.0 copy-start
  56.7 10.4 %patches.1.grad_ref = f32[2,4,128,1024]{3,2,1,0:T(8,128)} custom-call(f32[16,24,256]{2,1,0:T(8,128)} %now_ref.3, f32[16,24,256]{2,1,0:T(8,128)} %get-tuple-element.14.final_ref, s32[128]{0:T(128)} %bitcast.4, s32[1]{0:T(128)} %bitcast.3.cnt_ref, f32[8,128]{1,0:T(8,128)} %get-tuple-element.8.tot_ref, bf16[512,1024]{1,0:T(8,128)(2,1)} %win_ref.1, ...), custom_call_target="tpu_custom_call" | custom-call | tf_op jit(solution)/shard_map/patches/pallas_call | solution.py:470
  67.1 46.0 %reduce.1 = (f32[64,1024]{1,0:T(8,128)}, f32[128,512]{1,0:T(8,128)}) custom-call(f32[2,4,128,1024]{3,2,1,0:T(8,128)} %patches.1.grad_ref), custom_call_target="tpu_custom_call" | custom-call | tf_op jit(solution)/shard_map/reduce/pallas_call | solution.py:709
  113.1 0.0 copy-done
  113.1 0.7 copy.15
  113.8 1.7 %copy.16 = f32[64,1024]{1,0:T(8,128)} copy(f32[64,1024]{1,0:T(8,128)} %get-tuple-element.15) | data formatting | bytes 524288
  115.5 1.7 %copy.17 = f32[128,512]{1,0:T(8,128)} copy(f32[128,512]{1,0:T(8,128)} %get-tuple-element.16) | data formatting | bytes 524288
Async XLA Ops:
  56.7 56.4 %copy-start = (f32[16,24,256]{2,1,0:T(8,128)S(1)}, f32[16,24,256]{2,1,0:T(8,128)}, u32[]{:S(2)}) copy-start(f32[16,24,256]{2,1,0:T(8,128)} %get-tuple-element.14.final_ref) | copy-start | bytes 1179652

commit v2 on v0

v2 whole, which is shorter than its diff:
```python
import functools
import types

import jax
import jax.numpy as jnp
from jax import lax
from jax.experimental import pallas as pl
from jax.experimental.pallas import tpu as pltpu
from jax.sharding import PartitionSpec as P

STEPS = 8
PATCH = 8
LANES = 128
AXES = ("gx", "gy", "gz")
F32 = jnp.float32
BF16 = jnp.bfloat16


def remote(src, dst, send_sem, recv_sem, device):
    return pltpu.make_async_remote_copy(
        src_ref=src,
        dst_ref=dst,
        send_sem=send_sem,
        recv_sem=recv_sem,
        device_id=device,
        device_id_type=pl.DeviceIdType.MESH,
    )


def signal(sem, device):
    pl.semaphore_signal(
        sem, inc=1, device_id=device, device_id_type=pl.DeviceIdType.MESH
    )


def matmul(a, b, dims):
    return lax.dot_general(a, b, (dims, ((), ())), preferred_element_type=F32)


def in_order(values, order, parts):
    total = None
    rest = values
    for part in range(parts):
        piece = rest.astype(BF16)
        if part < parts - 1:
            rest = rest - piece.astype(F32)
        term = matmul(piece, order, ((1,), (0,)))
        total = term if total is None else total + term
    return total


def step_kernel(
    names,
    sizes,
    prev_ref,
    now_ref,
    mat_ref,
    tab_ref,
    cnt_ref,
    anchor_ref,
    win_hbm,
    wout_hbm,
    out_ref,
    sum_ref,
    *scratch,
):
    m = types.SimpleNamespace(**dict(zip(names, scratch)))
    nx, ny, nz = sizes
    gx, gy, gz = [lax.axis_index(axis) for axis in AXES]
    here = (gx, gy, gz)
    core, high = lax.rem(gx, 2), gx // 2
    low, y = lax.rem(gy, 2), gy // 2
    X, Y, Z = now_ref.shape
    W = Z + LANES
    T = W // LANES
    slots = anchor_ref.shape[0]
    wide, hidden = win_hbm.shape
    A, B, C = m.A, m.B, m.C

    def device(core=core, high=high, low=low, y=y, x=gz):
        return (high * 2 + core, y * 2 + low, x)

    def line_peer(axis, step):
        place = list(here)
        place[axis] = lax.rem(here[axis] + step, sizes[axis])
        return tuple(place)

    partner = device(core=1 - core)

    barrier = pltpu.get_barrier_semaphore()
    z_steps = [(h, l) for h in range(4) for l in range(2) if h or l]
    g_steps = [
        (i, j, l) for i in range(4) for j in range(4) for l in range(2) if i or j or l
    ]
    reached = []
    for axis in range(3):
        for step in range(1, sizes[axis]):
            reached.append(line_peer(axis, step))
    for dx in (nx - 1, 1):
        for dy in (ny - 1, 1):
            reached.append((lax.rem(gx + dx, nx), lax.rem(gy + dy, ny), gz))
    for h, l in z_steps:
        if h and l:
            reached.append(
                device(high=lax.rem(high + h, 4), low=lax.rem(low + l, 2))
            )
    for i, j, l in g_steps:
        if i and (j or l):
            reached.append(
                device(
                    x=lax.rem(gz + i, 4), y=lax.rem(y + j, 4), low=lax.rem(low + l, 2)
                )
            )

    load_in = pltpu.make_async_copy(win_hbm, m.w_in, m.load.at[0])
    load_out = pltpu.make_async_copy(wout_hbm, m.w_out, m.load.at[1])
    load_in.start()
    load_out.start()

    m.xrecv[...] = jnp.zeros(m.xrecv.shape, F32)
    m.yrecv[...] = jnp.zeros(m.yrecv.shape, F32)
    m.zrecv[...] = jnp.zeros(m.zrecv.shape, F32)
    m.crecv[...] = jnp.zeros(m.crecv.shape, F32)
    for place in reached:
        signal(barrier, place)

    lane = lax.broadcasted_iota(jnp.int32, (Y, LANES), 1)
    row = lax.broadcasted_iota(jnp.int32, (Y, W), 0)

    def put_rows(entry, x, value, tiles, first):
        for side, at in ((0, 0), (1, Y - 1)):
            for k, tile in enumerate(tiles):
                m.ysend[side, entry, tile, pl.ds(x, 1), :] = value[
                    at : at + 1, k * LANES : (k + 1) * LANES
                ]
                if first:
                    at2 = at + 1 - 2 * side
                    m.ysend[side, 1, tile, pl.ds(x, 1), :] = value[
                        at2 : at2 + 1, k * LANES : (k + 1) * LANES
                    ]

    inner_tiles = range(Z // LANES)
    last_tile = range(Z // LANES, T)

    def pack(x, carry):
        material = mat_ref[x]
        c = jnp.zeros((Y, Z), F32)
        for number in range(tab_ref.shape[0]):
            c = jnp.where(material == number, tab_ref[number], c)
        n, p = now_ref[x], prev_ref[x]
        C[x + 1, :, 0:Z] = c
        A[x + 2, :, 0:Z] = n
        B[x + 2, :, 0:Z] = p
        put_rows(0, x, n, inner_tiles, True)
        put_rows(2, x, p, inner_tiles, False)
        put_rows(3, x, c, inner_tiles, False)
        mine = lax.shift_right_logical(lane, 3) == x
        up, down = [], []
        for field, held_up, held_down in zip((n, p, c), carry[0], carry[1]):
            last = pltpu.roll(field[:, Z - LANES :], lax.rem(x * 8 + 8, LANES), 1)
            first = pltpu.roll(field[:, :LANES], x * 8, 1)
            up.append(jnp.where(mine, last, held_up))
            down.append(jnp.where(mine, first, held_down))
        return tuple(up), tuple(down)

    empty = tuple(jnp.zeros((Y, LANES), F32) for _ in range(3))
    ups, downs = lax.fori_loop(0, X, pack, (empty, empty))
    for i in range(3):
        m.zsend[0, i] = ups[i]
        m.zsend[1, i] = downs[i]

    def stage_planes(lanes):
        sources = (
            ((A, 2), (A, 3), (B, 2), (C, 1)),
            ((A, X), (A, X + 1), (B, X + 1), (C, X)),
        )
        for side in range(2):
            for entry, (field, plane) in enumerate(sources[side]):
                m.xsend[side, entry, :, lanes] = field[plane, :, lanes]

    main, edge = slice(0, Z), slice(Z, W)
    stage_planes(main)
    m.nsend[0] = jnp.full((8, LANES), cnt_ref[0].astype(F32))

    pl.semaphore_wait(barrier, len(reached))

    def z_copy(side):
        step = 1 if side == 0 else nz - 1
        return remote(
            m.zsend.at[side],
            m.zrecv.at[side],
            m.z_sem.at[0, side],
            m.z_sem.at[1, side],
            (gx, gy, lax.rem(gz + step, nz)),
        )

    @pl.when(gz < nz - 1)
    def _():
        z_copy(0).start()

    @pl.when(gz > 0)
    def _():
        z_copy(1).start()

    left, right = lax.rem(gx + nx - 1, nx), lax.rem(gx + 1, nx)
    below, above = lax.rem(gy + ny - 1, ny), lax.rem(gy + 1, ny)
    targets_of = (
        (left, gy, gz),
        (right, gy, gz),
        (gx, below, gz),
        (gx, above, gz),
        (left, below, gz),
        (left, above, gz),
        (right, below, gz),
        (right, above, gz),
    )
    sides = (gx > 0, gx < nx - 1, gy > 0, gy < ny - 1)
    has = sides + tuple(
        jnp.logical_and(sides[i], sides[j]) for i in (0, 1) for j in (2, 3)
    )
    opposite = (1, 0, 3, 2, 7, 6, 5, 4)

    def face(d, par, form):
        if d < 2:
            if form == 0:
                src = A.at[2:4] if d == 0 else A.at[X : X + 2]
                dst = m.xrecv.at[par, 1 - d, 0:2]
            else:
                lanes = pl.ds(0, Z) if form == 1 else pl.ds(Z, LANES)
                src = m.xsend.at[d, :, :, lanes]
                dst = m.xrecv.at[par, 1 - d, :, :, lanes]
        elif d < 4:
            side = d - 2
            if form == 0:
                src = m.ysend.at[side, 0:2]
                dst = m.yrecv.at[par, 1 - side, 0:2]
            else:
                tiles = pl.ds(0, T - 1) if form == 1 else pl.ds(T - 1, 1)
                src = m.ysend.at[side, :, tiles]
                dst = m.yrecv.at[par, 1 - side, :, tiles]
        else:
            src = m.csend.at[d - 4]
            dst = m.crecv.at[par, 7 - d]
        number = d + 8 if form == 2 else d
        arrives = opposite[d] + 8 if form == 2 else opposite[d]
        return remote(
            src, dst, m.f_send.at[number], m.f_recv.at[par, arrives], targets_of[d]
        )

    def each(ds, action):
        for d in ds:

            @pl.when(has[d])
            def _():
                action(d)

    def start(ds, par, form):
        each(ds, lambda d: face(d, par, form).start())

    def sent(ds, par, form):
        each(ds, lambda d: face(d, par, form).wait_send())

    def came(ds, par, form):
        each(ds, lambda d: face(opposite[d], par, form).wait_recv())

    start(range(4), 0, 1)

    def count_copy(axis, step):
        return remote(
            m.nsend.at[axis],
            m.nrecv.at[axis, here[axis]],
            m.n_send.at[axis, step],
            m.n_recv.at[axis, here[axis]],
            line_peer(axis, step),
        )

    def count_start(axis):
        for step in range(1, sizes[axis]):
            count_copy(axis, step).start()
        m.nrecv[axis, here[axis]] = m.nsend[axis]

    def count_finish(axis):
        size = sizes[axis]
        for step in range(1, size):
            count_copy(axis, step).wait_send()
            source = lax.rem(here[axis] + step, size)
            remote(
                m.nsend.at[axis],
                m.nrecv.at[axis, source],
                m.n_send.at[axis, step],
                m.n_recv.at[axis, source],
                line_peer(axis, step),
            ).wait_recv()
        total = m.nrecv[axis, 0]
        for i in range(1, size):
            total = total + m.nrecv[axis, i]
        return total

    count_start(0)

    tiles = X * Y // LANES
    narrow = lax.broadcasted_iota(jnp.int32, (8, LANES), 1)

    def turn(field):
        for x in range(X):
            for half in range(Z // LANES):
                m.rows[half, pl.ds(x, Y, stride=X), :] = field[
                    x, :, half * LANES : (half + 1) * LANES
                ]
        for half in range(Z // LANES):
            for tile in range(tiles):
                m.turned[tile, half * LANES : (half + 1) * LANES, :] = m.rows[
                    half, tile * LANES : (tile + 1) * LANES, :
                ].T

    def pick_one(s, tile, k, by):
        first = m.turned[tile, pl.ds(k, 8), :]
        second = m.turned[tile + 1, pl.ds(k, 8), :]
        back = lax.rem(LANES - by, LANES)
        m.picked[pl.ds(pl.multiple_of(s * 8, 8), 8), :] = jnp.where(
            narrow < LANES - by,
            pltpu.roll(first, back, 1),
            pltpu.roll(second, back, 1),
        )

    def pick_inputs(s, carry):
        anchor = anchor_ref[s]
        i = anchor // (Y * Z)
        j = lax.rem(anchor // Z, Y)
        k = lax.rem(anchor, Z)
        shift = j * X + i
        tile, by = shift // LANES, lax.rem(shift, LANES)
        m.where[0, s] = tile
        m.where[1, s] = k
        m.where[2, s] = by
        pick_one(s, tile, k, by)
        return carry

    def pick_targets(s, carry):
        pick_one(s, m.where[0, s], m.where[1, s], m.where[2, s])
        return carry

    def picked_values():
        return jnp.concatenate(
            [m.picked[pl.ds(c, slots, stride=8), :] for c in range(8)], axis=1
        )

    def swap(ref, number):
        return remote(
            ref.at[0:slots],
            ref.at[slots : 2 * slots],
            m.p_send.at[number],
            m.p_recv.at[number],
            partner,
        )

    m.turned[tiles] = jnp.zeros((Z, LANES), F32)
    turn(now_ref)

    @pl.when(gz < nz - 1)
    def _():
        z_copy(0).wait_send()
        z_copy(1).wait_recv()

    @pl.when(gz > 0)
    def _():
        z_copy(1).wait_send()
        z_copy(0).wait_recv()

    def unpack(x, carry):
        for i, (field, at) in enumerate(((A, 2), (B, 2), (C, 1))):
            before = pltpu.roll(m.zrecv[0, i], lax.rem(120 + LANES - x * 8, LANES), 1)
            after = pltpu.roll(m.zrecv[1, i], lax.rem(LANES - x * 8, LANES), 1)
            value = jnp.where(lane < 8, after, jnp.where(lane >= 120, before, 0.0))
            field[x + at, :, Z:W] = value
            put_rows((0, 2, 3)[i], x, value, last_tile, i == 0)
        return carry

    lax.fori_loop(0, X, unpack, 0)

    def put_lines():
        for i in range(4):
            plane = 2 if i < 2 else X + 1
            at = 0 if i % 2 == 0 else Y - 1
            m.csend[i] = A[plane, at : at + 1, :]

    stage_planes(edge)
    put_lines()
    start(range(4, 8), 0, 0)
    start(range(4), 0, 2)

    lax.fori_loop(0, slots, pick_inputs, 0, unroll=8)
    at = lax.broadcasted_iota(jnp.int32, (8 * LANES, wide), 0)
    feature = lax.broadcasted_iota(jnp.int32, (8 * LANES, wide), 1)
    pa = jnp.bitwise_and(at, X - 1)
    pb = jnp.bitwise_and(lax.shift_right_logical(at, 4), 7)
    pc = lax.shift_right_logical(at, 7)
    m.order[...] = jnp.where(
        (pa < PATCH) & (feature == pa * 64 + pb * 8 + pc), 1.0, 0.0
    ).astype(BF16)
    m.inputs[0:slots] = in_order(picked_values(), m.order[...], 3)
    swap(m.inputs, 0).start()

    root = 0.7978845608028654

    def forward(part):
        rows = slice(part * slots, (part + 1) * slots)
        inputs = m.inputs[rows]
        mean = jnp.mean(inputs * inputs, axis=1, keepdims=True)
        normed = (inputs * lax.rsqrt(mean + 1e-06)).astype(BF16)
        pre = matmul(normed, m.w_in[...], ((1,), (0,)))
        tanh = jnp.tanh(root * (pre + 0.044715 * (pre * pre * pre)))
        cdf = 0.5 * (1.0 + tanh)
        act = (pre * cdf).astype(BF16)
        m.act[rows] = act
        m.slope[rows] = cdf + 0.5 * pre * (1.0 - tanh * tanh) * (
            root * (1.0 + (3.0 * 0.044715) * (pre * pre))
        )
        m.base[rows] = inputs + matmul(act, m.w_out[...], ((1,), (0,)))
        source = lax.broadcasted_iota(jnp.int32, (wide, wide // 2), 0)
        column = lax.broadcasted_iota(jnp.int32, (wide, wide // 2), 1)
        block = lax.shift_right_logical(column, 6) * 2 + core
        chosen = jnp.where(
            source == block * 64 + jnp.bitwise_and(column, 63), 1.0, 0.0
        ).astype(BF16)
        m.normed[rows] = matmul(normed, chosen, ((1,), (0,))).astype(BF16)

    def backward(part, count):
        rows = slice(part * slots, (part + 1) * slots)
        err = m.base[rows] - m.targets[rows]
        slot = lax.broadcasted_iota(jnp.int32, (slots, 1), 0).astype(F32)
        valid = (slot < count).astype(F32)
        dout = (2.0 * err * valid / m.total[0:1, 0:1]).astype(BF16)
        m.dout[rows] = dout
        dact = matmul(dout, m.w_out[...], ((1,), (1,)))
        m.dpre[rows] = (dact * m.slope[rows]).astype(BF16)

    for r in range(STEPS // 2):
        par = r % 2
        if r == 0:
            came(range(4), 0, 1)
            came(range(4), 0, 2)
        else:
            came(range(4), par, 0)
        came(range(4, 8), par, 0)
        A[0:2] = m.xrecv[par, 0, 0:2]
        A[X + 2 : X + 4] = m.xrecv[par, 1, 0:2]
        if r == 0:
            B[1] = m.xrecv[0, 0, 2]
            B[X + 2] = m.xrecv[0, 1, 2]
            C[0] = m.xrecv[0, 0, 3]
            C[X + 1] = m.xrecv[0, 1, 3]
            m.yold[...] = m.yrecv[0, :, 2]
            m.ycoef[...] = m.yrecv[0, :, 3]

        def whole(parts):
            return jnp.concatenate(parts, axis=1)

        def update(field, plane, low_row, high_row, old, coef):
            n = field[plane]
            beside = field[plane + 1] + field[plane - 1]
            beside = beside + jnp.where(row == Y - 1, high_row, pltpu.roll(n, Y - 1, 0))
            beside = beside + jnp.where(row == 0, low_row, pltpu.roll(n, 1, 0))
            beside = beside + pltpu.roll(n, W - 1, 1) + pltpu.roll(n, 1, 1)
            return 2.0 * n - old + coef * (beside - 6.0 * n)

        def side_row(ref, index, x):
            return whole([ref[(*index, tile, pl.ds(x, 1), slice(None))] for tile in range(T)])

        def first(x, carry):
            B[x + 2] = update(
                A,
                x + 2,
                side_row(m.yrecv, (par, 0, 0), x),
                side_row(m.yrecv, (par, 1, 0), x),
                B[x + 2],
                C[x + 1],
            )
            return carry

        lax.fori_loop(0, X, first, 0)
        for plane, lines in ((1, (0, 1)), (X + 2, (2, 3))):
            B[plane] = update(
                A,
                plane,
                m.crecv[par, lines[0]],
                m.crecv[par, lines[1]],
                B[plane],
                C[plane - 1],
            )
        across = lax.broadcasted_iota(jnp.int32, (X, W), 0)
        for side in range(2):

            def plane_of(ref, *index):
                return whole([ref[(*index, tile)] for tile in range(T)])

            n = plane_of(m.yrecv, par, side, 0)
            outer = plane_of(m.yrecv, par, side, 1)
            inner = plane_of(m.ysend, side, 0)
            plus, minus = (inner, outer) if side == 0 else (outer, inner)
            beside = jnp.where(
                across == X - 1, m.crecv[par, 2 + side], pltpu.roll(n, X - 1, 0)
            )
            beside = beside + jnp.where(
                across == 0, m.crecv[par, side], pltpu.roll(n, 1, 0)
            )
            beside = beside + plus + minus
            beside = beside + pltpu.roll(n, W - 1, 1) + pltpu.roll(n, 1, 1)
            value = (
                2.0 * n
                - plane_of(m.yold, side)
                + plane_of(m.ycoef, side) * (beside - 6.0 * n)
            )
            for tile in range(T):
                m.yold[side, tile] = value[:, tile * LANES : (tile + 1) * LANES]
        if r == 0:
            sent(range(4), 0, 1)
            sent(range(4), 0, 2)
        else:
            sent(range(4), par, 0)
        sent(range(4, 8), par, 0)
        final_round = r == STEPS // 2 - 1

        def second(x, carry):
            after = update(
                B,
                x + 2,
                side_row(m.yold, (0,), x),
                side_row(m.yold, (1,), x),
                A[x + 2],
                C[x + 1],
            )
            if final_round:
                out_ref[x] = after[:, 0:Z]
            else:
                A[x + 2] = after
                put_rows(0, x, after, range(T), True)
            return carry

        lax.fori_loop(0, X, second, 0)
        if not final_round:
            put_lines()
            start(range(4, 8), 1 - par, 0)
            start(range(4), 1 - par, 0)
        if r == 0:
            load_in.wait()
            load_out.wait()
            forward(0)
            m.nsend[1] = count_finish(0)
            count_start(1)
        if r == 1:
            swap(m.inputs, 0).wait()
            forward(1)
            m.nsend[2] = count_finish(1)
            count_start(2)
        if r == 2:
            m.total[...] = count_finish(2)

    turn(out_ref)
    lax.fori_loop(0, slots, pick_targets, 0, unroll=8)
    m.targets[0:slots] = in_order(picked_values(), m.order[...], 2)
    swap(m.targets, 1).start()
    backward(0, m.nrecv[0, gx][0:1, 0:1])
    swap(m.targets, 1).wait()
    backward(1, m.nrecv[0, high * 2 + 1 - core][0:1, 0:1])
    grad_in = matmul(m.normed[...], m.dpre[...], ((0,), (0,)))
    dout = m.dout[...]
    for h in range(4):
        block = pl.multiple_of((h * 2 + core) * LANES, LANES)
        grad_out = matmul(m.act[:, pl.ds(block, LANES)], dout, ((0,), (0,)))
        m.sums[h, 0:64] = grad_in[h * 64 : (h + 1) * 64]
        m.sums[h, 64:128, 0:512] = grad_out[0:64]
        m.sums[h, 64:128, 512:1024] = grad_out[64:128]

    half = 512
    places = ((gz, lambda v: device(x=v)), (y, lambda v: device(y=v)))

    def ring(stage, colour, source, rows, relay, fin, send, sems):
        along = colour if stage == 0 else 1 - colour
        me, to = places[along]
        plus, minus, opposed = [lax.rem(me + d, 4) for d in (1, 3, 2)]

        def chunk(owner):
            return pl.ds(pl.multiple_of(owner * rows, 8), rows)

        begin, end = pl.ds(0, 2), pl.ds(2, 2)

        def piece(part, owner):
            return source(part, chunk(owner))

        def copy(src, dst, number, peer):
            return remote(
                src,
                dst,
                sems.at[colour, 0, number],
                sems.at[colour, 1, number],
                to(peer),
            )

        copies = [
            copy(piece(begin, opposed), relay.at[colour, 0], 0, plus),
            copy(piece(end, opposed), relay.at[colour, 1], 1, minus),
            copy(piece(end, plus), fin.at[colour, 0, end], 2, plus),
            copy(piece(begin, minus), fin.at[colour, 1, begin], 3, minus),
            copy(send.at[colour, 0], fin.at[colour, 0, begin], 4, plus),
            copy(send.at[colour, 1], fin.at[colour, 1, end], 5, minus),
        ]

        def open_ring():
            for one in copies[:4]:
                one.start()

        def pass_on():
            copies[0].wait_recv()
            send[colour, 0] = relay[colour, 0] + piece(begin, plus)[...]
            copies[4].start()
            copies[1].wait_recv()
            send[colour, 1] = relay[colour, 1] + piece(end, minus)[...]
            copies[5].start()

        def close_ring():
            for one in copies[2:]:
                one.wait_recv()
            own = piece(pl.ds(0, 4), me)[...]
            total = own + fin[colour, 0] + fin[colour, 1]
            for one in copies:
                one.wait_send()
            return total

        return open_ring, pass_on, close_ring

    def source1(colour):
        return lambda part, rows: m.sums.at[part, rows, pl.ds(colour * half, half)]

    def source2(colour):
        return lambda part, rows: m.held1.at[colour, part, rows, :]

    stage1 = [
        ring(0, colour, source1(colour), 32, m.relay1, m.fin1, m.send1, m.sems1)
        for colour in range(2)
    ]
    stage2 = [
        ring(1, colour, source2(colour), 8, m.relay2, m.fin2, m.send2, m.sems2)
        for colour in range(2)
    ]
    for rings, held in ((stage1, m.held1), (stage2, m.held2)):
        for one in rings:
            one[0]()
        for one in rings:
            one[1]()
        for colour, one in enumerate(rings):
            held[colour] = one[2]()

    z_me = high * 2 + low
    quarter = half // 2

    def z_piece(h, l):
        return m.held2.at[:, h, :, pl.ds(pl.multiple_of(l * quarter, quarter), quarter)]

    z_copies = []
    for number, (h, l) in enumerate(z_steps):
        ph, pw = lax.rem(high + h, 4), lax.rem(low + l, 2)
        peer = device(high=ph, low=pw)
        one = remote(
            z_piece(ph, pw),
            m.zgot.at[z_me],
            m.zp_send.at[number],
            m.zp_recv.at[z_me],
            peer,
        )
        one.start()
        z_copies.append((one, ph * 2 + pw, peer))
    m.zgot[z_me] = z_piece(high, low)[...]
    for one, slot, peer in z_copies:
        remote(
            z_piece(high, low),
            m.zgot.at[slot],
            m.zp_send.at[0],
            m.zp_recv.at[slot],
            peer,
        ).wait_recv()
    total = m.zgot[0]
    for slot in range(1, 8):
        total = total + m.zgot[slot]
    g_me = (gz * 4 + y) * 2 + low
    m.gathered[g_me] = total
    g_copies = []
    for number, (i, j, l) in enumerate(g_steps):
        px, py, pw = lax.rem(gz + i, 4), lax.rem(y + j, 4), lax.rem(low + l, 2)
        peer = device(x=px, y=py, low=pw)
        one = remote(
            m.gathered.at[g_me],
            m.gathered.at[g_me],
            m.g_send.at[number],
            m.g_recv.at[g_me],
            peer,
        )
        one.start()
        g_copies.append((one, (px * 4 + py) * 2 + pw, peer))
    for one, slot, peer in z_copies:
        one.wait_send()
    for one, slot, peer in g_copies:
        remote(
            m.gathered.at[slot],
            m.gathered.at[slot],
            m.g_send.at[0],
            m.g_recv.at[slot],
            peer,
        ).wait_recv()
    sum_ref[...] = m.gathered[...]
    for one, slot, peer in g_copies:
        one.wait_send()


def step(prev, now, material, table, used, anchors, w_in, w_out, sizes):
    X, Y, Z = now.shape
    W = Z + LANES
    T = W // LANES
    slots = anchors.shape[0]
    wide, hidden = w_in.shape
    vmem = pl.BlockSpec(memory_space=pltpu.VMEM)
    smem = pl.BlockSpec(memory_space=pltpu.SMEM)
    anywhere = pl.BlockSpec(memory_space=pl.ANY)
    dma = pltpu.SemaphoreType.DMA
    most = max(sizes)

    def f32(*shape):
        return pltpu.VMEM(shape, F32)

    def b16(*shape):
        return pltpu.VMEM(shape, BF16)

    scratch = dict(
        A=f32(X + 4, Y, W),
        B=f32(X + 4, Y, W),
        C=f32(X + 2, Y, W),
        xsend=f32(2, 4, Y, W),
        xrecv=f32(2, 2, 4, Y, W),
        ysend=f32(2, 4, T, X, LANES),
        yrecv=f32(2, 2, 4, T, X, LANES),
        yold=f32(2, T, X, LANES),
        ycoef=f32(2, T, X, LANES),
        csend=f32(4, 1, W),
        crecv=f32(2, 4, 1, W),
        zsend=f32(2, 3, Y, LANES),
        zrecv=f32(2, 3, Y, LANES),
        nsend=f32(3, 8, LANES),
        nrecv=f32(3, most, 8, LANES),
        total=f32(8, LANES),
        rows=f32(Z // LANES, X * Y, LANES),
        turned=f32(X * Y // LANES + 1, Z, LANES),
        picked=f32(8 * slots, LANES),
        where=pltpu.SMEM((3, slots), jnp.int32),
        order=b16(8 * LANES, wide),
        w_in=b16(wide, hidden),
        w_out=b16(hidden, wide),
        inputs=f32(2 * slots, wide),
        targets=f32(2 * slots, wide),
        base=f32(2 * slots, wide),
        normed=b16(2 * slots, wide // 2),
        act=b16(2 * slots, hidden),
        slope=f32(2 * slots, hidden),
        dout=b16(2 * slots, wide),
        dpre=b16(2 * slots, hidden),
        sums=f32(4, 128, 1024),
        relay1=f32(2, 2, 2, 32, 512),
        fin1=f32(2, 2, 4, 32, 512),
        send1=f32(2, 2, 2, 32, 512),
        held1=f32(2, 4, 32, 512),
        relay2=f32(2, 2, 2, 8, 512),
        fin2=f32(2, 2, 4, 8, 512),
        send2=f32(2, 2, 2, 8, 512),
        held2=f32(2, 4, 8, 512),
        zgot=f32(8, 2, 8, 256),
        gathered=f32(32, 2, 8, 256),
        load=dma((2,)),
        z_sem=dma((2, 2)),
        f_send=dma((12,)),
        f_recv=dma((2, 12)),
        n_send=dma((3, most)),
        n_recv=dma((3, most)),
        p_send=dma((2,)),
        p_recv=dma((2,)),
        sems1=dma((2, 2, 6)),
        sems2=dma((2, 2, 6)),
        zp_send=dma((7,)),
        zp_recv=dma((8,)),
        g_send=dma((31,)),
        g_recv=dma((32,)),
    )
    return pl.pallas_call(
        functools.partial(step_kernel, tuple(scratch), sizes),
        name="step",
        out_shape=(
            jax.ShapeDtypeStruct((X, Y, Z), F32),
            jax.ShapeDtypeStruct((32, 2, 8, 256), F32),
        ),
        in_specs=[vmem, vmem, vmem, smem, smem, smem, anywhere, anywhere],
        out_specs=(vmem, vmem),
        scratch_shapes=list(scratch.values()),
        compiler_params=pltpu.CompilerParams(
            collective_id=0,
            has_side_effects=True,
            vmem_limit_bytes=48 * 1024 * 1024,
        ),
    )(prev, now, material, table, used, anchors, w_in, w_out)


def place_kernel(final_ref, sum_ref, final_out, in_ref, out_ref):
    final_out[...] = final_ref[...]
    for slot in range(32):
        ix, iy, il = slot // 8, slot // 2 % 4, slot % 2
        for colour in range(2):
            row = ix * 32 + iy * 8 if colour == 0 else iy * 32 + ix * 8
            at = colour * 512 + il * 256
            value = sum_ref[slot, colour]
            if row < 64:
                in_ref[row : row + 8, at : at + 256] = value
            else:
                top = row - 64 + (64 if at >= 512 else 0)
                left = at % 512
                out_ref[top : top + 8, left : left + 256] = value


def place(final, sums):
    vmem = pl.BlockSpec(memory_space=pltpu.VMEM)
    return pl.pallas_call(
        place_kernel,
        name="place",
        out_shape=(
            jax.ShapeDtypeStruct(final.shape, F32),
            jax.ShapeDtypeStruct((64, 1024), F32),
            jax.ShapeDtypeStruct((128, 512), F32),
        ),
        in_specs=[vmem, vmem],
        out_specs=(vmem, vmem, vmem),
    )(final, sums)


def body(pressure_prev, pressure_now, material, speed_table, anchors, counts, w_in, w_out):
    sizes = tuple(lax.axis_size(axis) for axis in AXES)
    final, sums = step(
        pressure_prev,
        pressure_now,
        material,
        speed_table,
        counts.reshape(-1),
        anchors.reshape(-1),
        w_in,
        w_out,
        sizes,
    )
    return place(final, sums)


def solution(mesh):
    return jax.shard_map(
        body,
        mesh=mesh,
        in_specs=(
            P("gx", "gy", "gz"),
            P("gx", "gy", "gz"),
            P("gx", "gy", "gz"),
            P(),
            P("gx", "gy", "gz"),
            P("gx", "gy", "gz"),
            P(),
            P(),
        ),
        out_specs=(P("gx", "gy", "gz"), P("gx", None), P("gx", None)),
        check_vma=False,
    )
```

time: 1380 us -> 97.4 us (0.07)
  local copies, waits for them, and re-layouts: 735 us -> 7.63 us
  waiting for transfers between devices: 332 us -> 0 us
  starting transfers between devices: 152 us -> 0 us
  Pallas kernels: 0 us -> 88.2 us
  blocking collectives: 83.4 us -> 0 us
  other arithmetic: 50.9 us -> 0 us
  between operations: 15.7 us -> 1.32 us
    gather x4 -> x0, local copies, waits for them, and re-layouts: 725 us -> none  [the longest x2 363 us: body(): inputs = jnp.take(pressure_now.reshape(-1), cell_index, axis=0)]
    psum x1 -> x0, waiting for transfers between devices: 271 us -> none  [body(): summed_in, summed_out = lax.psum((full_in, full_out), ('gx', 'gy', 'gz'))]
    ppermute x48 -> x0, starting transfers between devices: 152 us -> none  [the longest x24 113 us: extended(): before = lax.ppermute(last, axis, up)]
    pallas_call x0 -> x2, Pallas kernels: none -> 88.2 us  [the longest x1 86.1 us: step(): pl.pallas_call(functools.partial(step_kernel, tuple(scratch), sizes), nam...]
    psum x1 -> x0, blocking collectives: 83.4 us -> none  [body(): total = lax.psum(used.astype(jnp.float32), ('gx', 'gy', 'gz'))]
    ppermute x48 -> x0, waiting for transfers between devices: 61.1 us -> none  [the longest x24 35.3 us: extended(): before = lax.ppermute(last, axis, up)]
    add x10 -> x0, other arithmetic: 48.2 us -> none  [the longest x8 48.1 us: update(): return 2.0 * now - prev + coef * (beside - 6.0 * now)]
  transfers between devices with their start and end apart: 49 -> 0, of which waited for: 30 -> 0; matrix products, arithmetic and copies ran while one was open for 27% -> 0% of each run, Pallas kernels for 0% -> 0%
where the time goes in v2:
time: 97.4 us; the launch traced here: 97.1 us
  Pallas kernels  88.2 us (91%)
  local copies, waits for them, and re-layouts  7.63 us (8%)
  between operations  1.32 us (1%)
    pallas_call x1, Pallas kernels, step(): pl.pallas_call(functools.partial(step_kernel, tuple(scratch), sizes), nam...  86.1 us
    unnamed x18, local copies, waits for them, and re-layouts  7.63 us
    pallas_call x1, Pallas kernels, place(): pl.pallas_call(place_kernel, name='place', out_shape=(jax.ShapeDtypeStruc...  2.1 us

profile of v2, /device:TPU:8, one launch (start us, length us, event | category | flops | bytes accessed | tf_op | source)
XLA Modules:
  0.0 97.1 jit_solution(4963727772895346404)
XLA Ops:
  1.3 0.0 copy-start.7
  1.3 0.0 copy-start.8
  1.3 0.6 copy-done.7
  1.9 0.0 copy-done.8
  2.0 0.0 copy-start
  2.0 1.2 %copy-done = bf16[512,1024]{1,0:T(8,128)(2,1)S(1)} copy-done((bf16[512,1024]{1,0:T(8,128)(2,1)S(1)}, bf16[512,1024]{1,0:T(8,128)(2,1)}, u32[]{:S(2)}) %copy-start) | copy-done | bytes 1048600
  3.2 0.0 copy-start.1
  3.2 1.2 %copy-done.1 = bf16[1024,512]{1,0:T(8,128)(2,1)S(1)} copy-done((bf16[1024,512]{1,0:T(8,128)(2,1)S(1)}, bf16[1024,512]{1,0:T(8,128)(2,1)}, u32[]{:S(2)}) %copy-start.1) | copy-done | bytes 1048600
  4.4 0.0 copy-start.3
  4.4 1.0 %copy-done.3 = f32[16,24,256]{2,1,0:T(8,128)S(1)} copy-done((f32[16,24,256]{2,1,0:T(8,128)S(1)}, f32[16,24,256]{2,1,0:T(8,128)}, u32[]{:S(2)}) %copy-start.3) | copy-done | bytes 393240
  5.4 0.0 copy-start.4
  5.4 1.0 %copy-done.4 = f32[16,24,256]{2,1,0:T(8,128)S(1)} copy-done((f32[16,24,256]{2,1,0:T(8,128)S(1)}, f32[16,24,256]{2,1,0:T(8,128)}, u32[]{:S(2)}) %copy-start.4) | copy-done | bytes 393240
  6.4 0.0 copy-start.5
  6.4 1.0 %copy-done.5 = s32[16,24,256]{2,1,0:T(8,128)S(1)} copy-done((s32[16,24,256]{2,1,0:T(8,128)S(1)}, s32[16,24,256]{2,1,0:T(8,128)}, u32[]{:S(2)}) %copy-start.5) | copy-done | bytes 393240
  7.4 86.1 %step.1 = (f32[16,24,256]{2,1,0:T(8,128)S(1)}, f32[32,2,8,256]{3,2,1,0:T(8,128)S(1)}) custom-call(f32[16,24,256]{2,1,0:T(8,128)S(1)} %copy-done.3, f32[16,24,256]{2,1,0:T(8,128)S(1)} %copy-done.4, s32[16,24,256]{2,1,0:T(8,128)S(1)} %copy-done.5, f32[8]{0:T(128)S(1)} %copy-done.7, s32[1]{0:T(128)} %bitcast.2.cnt_ref, s32[128]{0:T(128)S(1)} %bitcast.3, ...), custom_call_target="tpu_custom_call" | custom-call | tf_op jit(solution)/shard_map/step/pallas_call | solution.py:791
  93.5 0.0 copy-start.2
  93.5 0.8 copy-done.2
  94.3 0.0 copy-start.6
  94.3 0.7 copy-done.6
  95.0 2.1 %place.1 = (f32[16,24,256]{2,1,0:T(8,128)}, f32[64,1024]{1,0:T(8,128)}, f32[128,512]{1,0:T(8,128)}) custom-call(f32[16,24,256]{2,1,0:T(8,128)} %copy-done.6, f32[32,2,8,256]{3,2,1,0:T(8,128)} %copy-done.2), custom_call_target="tpu_custom_call" | custom-call | tf_op jit(solution)/shard_map/place/pallas_call | solution.py:827
Async XLA Ops:
  1.3 0.7 copy-start.7
  1.3 0.7 copy-start.8
  2.0 1.2 %copy-start = (bf16[512,1024]{1,0:T(8,128)(2,1)S(1)}, bf16[512,1024]{1,0:T(8,128)(2,1)}, u32[]{:S(2)}) copy-start(bf16[512,1024]{1,0:T(8,128)(2,1)} %win_hbm.1) | copy-start | bytes 3145732
  3.2 1.2 %copy-start.1 = (bf16[1024,512]{1,0:T(8,128)(2,1)S(1)}, bf16[1024,512]{1,0:T(8,128)(2,1)}, u32[]{:S(2)}) copy-start(bf16[1024,512]{1,0:T(8,128)(2,1)} %wout_hbm.1) | copy-start | bytes 3145732
  4.4 1.0 %copy-start.3 = (f32[16,24,256]{2,1,0:T(8,128)S(1)}, f32[16,24,256]{2,1,0:T(8,128)}, u32[]{:S(2)}) copy-start(f32[16,24,256]{2,1,0:T(8,128)} %prev_ref.1) | copy-start | bytes 1179652
  5.4 1.0 %copy-start.4 = (f32[16,24,256]{2,1,0:T(8,128)S(1)}, f32[16,24,256]{2,1,0:T(8,128)}, u32[]{:S(2)}) copy-start(f32[16,24,256]{2,1,0:T(8,128)} %now_ref.1) | copy-start | bytes 1179652
  6.4 1.0 %copy-start.5 = (s32[16,24,256]{2,1,0:T(8,128)S(1)}, s32[16,24,256]{2,1,0:T(8,128)}, u32[]{:S(2)}) copy-start(s32[16,24,256]{2,1,0:T(8,128)} %mat_ref.1) | copy-start | bytes 1179652
  93.5 0.8 copy-start.2
  94.3 0.7 copy-start.6

commit v3 on v2

--- a/solution.py
+++ b/solution.py
@@ -52,9 +52,9 @@
 def step_kernel(
     names,
     sizes,
-    prev_ref,
-    now_ref,
-    mat_ref,
+    prev_hbm,
+    now_hbm,
+    mat_hbm,
     tab_ref,
     cnt_ref,
     anchor_ref,
@@ -70,7 +70,7 @@
     here = (gx, gy, gz)
     core, high = lax.rem(gx, 2), gx // 2
     low, y = lax.rem(gy, 2), gy // 2
-    X, Y, Z = now_ref.shape
+    X, Y, Z = now_hbm.shape
     W = Z + LANES
     T = W // LANES
     slots = anchor_ref.shape[0]
@@ -112,6 +112,14 @@
                 )
             )
 
+    bricks = (slice(2, X + 2), slice(None), slice(0, Z))
+    loads = [
+        pltpu.make_async_copy(mat_hbm, m.mat, m.load.at[2]),
+        pltpu.make_async_copy(now_hbm, A.at[bricks], m.load.at[3]),
+        pltpu.make_async_copy(prev_hbm, B.at[bricks], m.load.at[4]),
+    ]
+    for one in loads:
+        one.start()
     load_in = pltpu.make_async_copy(win_hbm, m.w_in, m.load.at[0])
     load_out = pltpu.make_async_copy(wout_hbm, m.w_out, m.load.at[1])
     load_in.start()
@@ -142,15 +150,16 @@
     inner_tiles = range(Z // LANES)
     last_tile = range(Z // LANES, T)
 
+    for one in loads:
+        one.wait()
+
     def pack(x, carry):
-        material = mat_ref[x]
+        material = m.mat[x]
         c = jnp.zeros((Y, Z), F32)
         for number in range(tab_ref.shape[0]):
             c = jnp.where(material == number, tab_ref[number], c)
-        n, p = now_ref[x], prev_ref[x]
+        n, p = A[x + 2, :, 0:Z], B[x + 2, :, 0:Z]
         C[x + 1, :, 0:Z] = c
-        A[x + 2, :, 0:Z] = n
-        B[x + 2, :, 0:Z] = p
         put_rows(0, x, n, inner_tiles, True)
         put_rows(2, x, p, inner_tiles, False)
         put_rows(3, x, c, inner_tiles, False)
@@ -301,11 +310,11 @@
     tiles = X * Y // LANES
     narrow = lax.broadcasted_iota(jnp.int32, (8, LANES), 1)
 
-    def turn(field):
+    def turn(field, first):
         for x in range(X):
             for half in range(Z // LANES):
                 m.rows[half, pl.ds(x, Y, stride=X), :] = field[
-                    x, :, half * LANES : (half + 1) * LANES
+                    x + first, :, half * LANES : (half + 1) * LANES
                 ]
         for half in range(Z // LANES):
             for tile in range(tiles):
@@ -355,7 +364,7 @@
         )
 
     m.turned[tiles] = jnp.zeros((Z, LANES), F32)
-    turn(now_ref)
+    turn(A, 2)
 
     @pl.when(gz < nz - 1)
     def _():
@@ -556,7 +565,7 @@
         if r == 2:
             m.total[...] = count_finish(2)
 
-    turn(out_ref)
+    turn(out_ref, 0)
     lax.fori_loop(0, slots, pick_targets, 0, unroll=8)
     m.targets[0:slots] = in_order(picked_values(), m.order[...], 2)
     swap(m.targets, 1).start()
@@ -720,7 +729,7 @@
     wide, hidden = w_in.shape
     vmem = pl.BlockSpec(memory_space=pltpu.VMEM)
     smem = pl.BlockSpec(memory_space=pltpu.SMEM)
-    anywhere = pl.BlockSpec(memory_space=pl.ANY)
+    hbm = pl.BlockSpec(memory_space=pltpu.HBM)
     dma = pltpu.SemaphoreType.DMA
     most = max(sizes)
 
@@ -750,6 +759,7 @@
         rows=f32(Z // LANES, X * Y, LANES),
         turned=f32(X * Y // LANES + 1, Z, LANES),
         picked=f32(8 * slots, LANES),
+        mat=pltpu.VMEM((X, Y, Z), jnp.int32),
         where=pltpu.SMEM((3, slots), jnp.int32),
         order=b16(8 * LANES, wide),
         w_in=b16(wide, hidden),
@@ -773,7 +783,7 @@
         held2=f32(2, 4, 8, 512),
         zgot=f32(8, 2, 8, 256),
         gathered=f32(32, 2, 8, 256),
-        load=dma((2,)),
+        load=dma((5,)),
         z_sem=dma((2, 2)),
         f_send=dma((12,)),
         f_recv=dma((2, 12)),
@@ -795,13 +805,13 @@
             jax.ShapeDtypeStruct((X, Y, Z), F32),
             jax.ShapeDtypeStruct((32, 2, 8, 256), F32),
         ),
-        in_specs=[vmem, vmem, vmem, smem, smem, smem, anywhere, anywhere],
+        in_specs=[hbm, hbm, hbm, smem, smem, smem, hbm, hbm],
         out_specs=(vmem, vmem),
         scratch_shapes=list(scratch.values()),
         compiler_params=pltpu.CompilerParams(
             collective_id=0,
             has_side_effects=True,
-            vmem_limit_bytes=48 * 1024 * 1024,
+            vmem_limit_bytes=40 * 1024 * 1024,
         ),
     )(prev, now, material, table, used, anchors, w_in, w_out)
 
@@ -834,18 +844,31 @@
         ),
         in_specs=[vmem, vmem],
         out_specs=(vmem, vmem, vmem),
+        compiler_params=pltpu.CompilerParams(vmem_limit_bytes=8 * 1024 * 1024),
     )(final, sums)
 
 
 def body(pressure_prev, pressure_now, material, speed_table, anchors, counts, w_in, w_out):
     sizes = tuple(lax.axis_size(axis) for axis in AXES)
+    pressure_prev, pressure_now, material, speed_table, anchors, w_in, w_out = [
+        pltpu.with_memory_space_constraint(v, pltpu.HBM)
+        for v in (
+            pressure_prev,
+            pressure_now,
+            material,
+            speed_table,
+            anchors.reshape(-1),
+            w_in,
+            w_out,
+        )
+    ]
     final, sums = step(
         pressure_prev,
         pressure_now,
         material,
         speed_table,
         counts.reshape(-1),
-        anchors.reshape(-1),
+        anchors,
         w_in,
         w_out,
         sizes,

time: 97.4 us -> 88.5 us (0.909)
  local copies, waits for them, and re-layouts: 7.63 us -> 0 us
  Pallas kernels: 88.2 us -> 87.2 us
    unnamed x18 -> x0, local copies, waits for them, and re-layouts: 7.63 us -> none
    pallas_call x1, Pallas kernels: 2.1 us -> 0.98 us  [place(): pl.pallas_call(place_kernel, name='place', out_shape=(jax.ShapeDtypeStruc...]
where the time goes in v3:
time: 88.5 us; the launch traced here: 88.4 us
  Pallas kernels  87.2 us (99%)
  between operations  1.29 us (1%)
    pallas_call x1, Pallas kernels, step(): pl.pallas_call(functools.partial(step_kernel, tuple(scratch), sizes), nam...  86.2 us

profile of v3, /device:TPU:8, one launch (start us, length us, event | category | flops | bytes accessed | tf_op | source)
XLA Modules:
  0.0 88.4 jit_solution(2854078146873684209)
XLA Ops:
  1.3 86.2 %step.1 = (f32[16,24,256]{2,1,0:T(8,128)S(1)}, f32[32,2,8,256]{3,2,1,0:T(8,128)S(1)}) custom-call(f32[16,24,256]{2,1,0:T(8,128)} %prev_hbm.1, f32[16,24,256]{2,1,0:T(8,128)} %now_hbm.1, s32[16,24,256]{2,1,0:T(8,128)} %mat_hbm.1, f32[8]{0:T(128)} %tab_ref.1, s32[1]{0:T(128)} %bitcast.2.cnt_ref, s32[128]{0:T(128)} %bitcast.3, bf16[512,1024]{1,0:T(8,128)(2,1)} %win_hbm.1, ...), custom_call_target="tpu_custom_call" | custom-call | tf_op jit(solution)/shard_map/step/pallas_call | solution.py:801
  87.5 1.0 %place.1 = (f32[16,24,256]{2,1,0:T(8,128)}, f32[64,1024]{1,0:T(8,128)}, f32[128,512]{1,0:T(8,128)}) custom-call(f32[16,24,256]{2,1,0:T(8,128)S(1)} %get-tuple-element.5.final_ref, f32[32,2,8,256]{3,2,1,0:T(8,128)S(1)} %get-tuple-element.6.sum_ref), custom_call_target="tpu_custom_call" | custom-call | tf_op jit(solution)/shard_map/place/pallas_call | solution.py:837

commit v4 on v3

--- a/solution.py
+++ b/solution.py
@@ -11,6 +11,8 @@
 STEPS = 8
 PATCH = 8
 LANES = 128
+R = 32
+PAD = 8
 AXES = ("gx", "gy", "gz")
 F32 = jnp.float32
 BF16 = jnp.bfloat16
@@ -75,7 +77,29 @@
     T = W // LANES
     slots = anchor_ref.shape[0]
     wide, hidden = win_hbm.shape
-    A, B, C = m.A, m.B, m.C
+    A, B, C, D = m.A, m.B, m.C, m.D
+
+    def rows_of(p, t, shift=0, count=Y):
+        start = p * (T * R) + (PAD + t * R)
+        if not isinstance(p, int):
+            start = pl.multiple_of(start, 8)
+        return pl.ds(start + shift, count)
+
+    def rows_over(t, shift):
+        return pl.ds(2 * T * R + PAD + t * R + shift, X, stride=T * R)
+
+    def coef_of(p, t):
+        start = p * (T * Y) + t * Y
+        if not isinstance(p, int):
+            start = pl.multiple_of(start, 8)
+        return pl.ds(start, Y)
+
+    def coef_over(t, shift):
+        return pl.ds(T * Y + t * Y + shift, X, stride=T * Y)
+
+    def tile_of(t):
+        return slice(t * LANES, (t + 1) * LANES)
+
 
     def device(core=core, high=high, low=low, y=y, x=gz):
         return (high * 2 + core, y * 2 + low, x)
@@ -112,11 +136,10 @@
                 )
             )
 
-    bricks = (slice(2, X + 2), slice(None), slice(0, Z))
     loads = [
         pltpu.make_async_copy(mat_hbm, m.mat, m.load.at[2]),
-        pltpu.make_async_copy(now_hbm, A.at[bricks], m.load.at[3]),
-        pltpu.make_async_copy(prev_hbm, B.at[bricks], m.load.at[4]),
+        pltpu.make_async_copy(now_hbm, m.now, m.load.at[3]),
+        pltpu.make_async_copy(prev_hbm, m.prev, m.load.at[4]),
     ]
     for one in loads:
         one.start()
@@ -133,19 +156,23 @@
         signal(barrier, place)
 
     lane = lax.broadcasted_iota(jnp.int32, (Y, LANES), 1)
-    row = lax.broadcasted_iota(jnp.int32, (Y, W), 0)
-
-    def put_rows(entry, x, value, tiles, first):
-        for side, at in ((0, 0), (1, Y - 1)):
-            for k, tile in enumerate(tiles):
-                m.ysend[side, entry, tile, pl.ds(x, 1), :] = value[
-                    at : at + 1, k * LANES : (k + 1) * LANES
-                ]
-                if first:
-                    at2 = at + 1 - 2 * side
-                    m.ysend[side, 1, tile, pl.ds(x, 1), :] = value[
-                        at2 : at2 + 1, k * LANES : (k + 1) * LANES
-                    ]
+    def put_rows(entries, tiles):
+        for side, at, second in ((0, 0, 1), (1, Y - 1, Y - 2)):
+            for t in tiles:
+                m.ysend[side, 0, t] = A[rows_over(t, at), :]
+                m.ysend[side, 1, t] = A[rows_over(t, second), :]
+                if entries > 2:
+                    m.ysend[side, 2, t] = B[rows_over(t, at), :]
+                    m.ysend[side, 3, t] = C[coef_over(t, at), :]
+
+    def put_planes(entries, tiles):
+        for side, planes in enumerate(((2, 3, 2, 1), (X, X + 1, X + 1, X))):
+            for t in tiles:
+                m.xsend[side, 0, t] = A[rows_of(planes[0], t), :]
+                m.xsend[side, 1, t] = A[rows_of(planes[1], t), :]
+                if entries > 2:
+                    m.xsend[side, 2, t] = B[rows_of(planes[2], t), :]
+                    m.xsend[side, 3, t] = C[coef_of(planes[3], t), :]
 
     inner_tiles = range(Z // LANES)
     last_tile = range(Z // LANES, T)
@@ -158,11 +185,12 @@
         c = jnp.zeros((Y, Z), F32)
         for number in range(tab_ref.shape[0]):
             c = jnp.where(material == number, tab_ref[number], c)
-        n, p = A[x + 2, :, 0:Z], B[x + 2, :, 0:Z]
-        C[x + 1, :, 0:Z] = c
-        put_rows(0, x, n, inner_tiles, True)
-        put_rows(2, x, p, inner_tiles, False)
-        put_rows(3, x, c, inner_tiles, False)
+        n, p = m.now[x], m.prev[x]
+        for t in inner_tiles:
+            A[rows_of(x + 2, t), :] = n[:, tile_of(t)]
+            B[rows_of(x + 2, t), :] = p[:, tile_of(t)]
+            C[coef_of(x + 1, t), :] = c[:, tile_of(t)]
+            D[coef_of(x + 1, t), :] = 2.0 - 6.0 * c[:, tile_of(t)]
         mine = lax.shift_right_logical(lane, 3) == x
         up, down = [], []
         for field, held_up, held_down in zip((n, p, c), carry[0], carry[1]):
@@ -178,17 +206,8 @@
         m.zsend[0, i] = ups[i]
         m.zsend[1, i] = downs[i]
 
-    def stage_planes(lanes):
-        sources = (
-            ((A, 2), (A, 3), (B, 2), (C, 1)),
-            ((A, X), (A, X + 1), (B, X + 1), (C, X)),
-        )
-        for side in range(2):
-            for entry, (field, plane) in enumerate(sources[side]):
-                m.xsend[side, entry, :, lanes] = field[plane, :, lanes]
-
-    main, edge = slice(0, Z), slice(Z, W)
-    stage_planes(main)
+    put_planes(4, inner_tiles)
+    put_rows(4, inner_tiles)
     m.nsend[0] = jnp.full((8, LANES), cnt_ref[0].astype(F32))
 
     pl.semaphore_wait(barrier, len(reached))
@@ -232,12 +251,12 @@
     def face(d, par, form):
         if d < 2:
             if form == 0:
-                src = A.at[2:4] if d == 0 else A.at[X : X + 2]
+                src = m.xsend.at[d, 0:2]
                 dst = m.xrecv.at[par, 1 - d, 0:2]
             else:
-                lanes = pl.ds(0, Z) if form == 1 else pl.ds(Z, LANES)
-                src = m.xsend.at[d, :, :, lanes]
-                dst = m.xrecv.at[par, 1 - d, :, :, lanes]
+                tiles = pl.ds(0, T - 1) if form == 1 else pl.ds(T - 1, 1)
+                src = m.xsend.at[d, :, tiles]
+                dst = m.xrecv.at[par, 1 - d, :, tiles]
         elif d < 4:
             side = d - 2
             if form == 0:
@@ -310,11 +329,11 @@
     tiles = X * Y // LANES
     narrow = lax.broadcasted_iota(jnp.int32, (8, LANES), 1)
 
-    def turn(field, first):
+    def turn(field):
         for x in range(X):
             for half in range(Z // LANES):
                 m.rows[half, pl.ds(x, Y, stride=X), :] = field[
-                    x + first, :, half * LANES : (half + 1) * LANES
+                    x, :, half * LANES : (half + 1) * LANES
                 ]
         for half in range(Z // LANES):
             for tile in range(tiles):
@@ -364,7 +383,7 @@
         )
 
     m.turned[tiles] = jnp.zeros((Z, LANES), F32)
-    turn(A, 2)
+    turn(m.now)
 
     @pl.when(gz < nz - 1)
     def _():
@@ -377,23 +396,30 @@
         z_copy(0).wait_recv()
 
     def unpack(x, carry):
-        for i, (field, at) in enumerate(((A, 2), (B, 2), (C, 1))):
+        values = []
+        for i in range(3):
             before = pltpu.roll(m.zrecv[0, i], lax.rem(120 + LANES - x * 8, LANES), 1)
             after = pltpu.roll(m.zrecv[1, i], lax.rem(LANES - x * 8, LANES), 1)
-            value = jnp.where(lane < 8, after, jnp.where(lane >= 120, before, 0.0))
-            field[x + at, :, Z:W] = value
-            put_rows((0, 2, 3)[i], x, value, last_tile, i == 0)
+            values.append(
+                jnp.where(lane < 8, after, jnp.where(lane >= 120, before, 0.0))
+            )
+        A[rows_of(x + 2, T - 1), :] = values[0]
+        B[rows_of(x + 2, T - 1), :] = values[1]
+        C[coef_of(x + 1, T - 1), :] = values[2]
+        D[coef_of(x + 1, T - 1), :] = 2.0 - 6.0 * values[2]
         return carry
 
-    lax.fori_loop(0, X, unpack, 0)
+    lax.fori_loop(0, X, unpack, 0, unroll=2)
 
     def put_lines():
         for i in range(4):
             plane = 2 if i < 2 else X + 1
             at = 0 if i % 2 == 0 else Y - 1
-            m.csend[i] = A[plane, at : at + 1, :]
-
-    stage_planes(edge)
+            for t in range(T):
+                m.csend[i, :, tile_of(t)] = A[rows_of(plane, t, at, 1), :]
+
+    put_planes(4, last_tile)
+    put_rows(4, last_tile)
     put_lines()
     start(range(4, 8), 0, 0)
     start(range(4), 0, 2)
@@ -452,51 +478,52 @@
         else:
             came(range(4), par, 0)
         came(range(4, 8), par, 0)
-        A[0:2] = m.xrecv[par, 0, 0:2]
-        A[X + 2 : X + 4] = m.xrecv[par, 1, 0:2]
+        for t in range(T):
+            for e in range(2):
+                A[rows_of(e, t), :] = m.xrecv[par, 0, e, t]
+                A[rows_of(X + 2 + e, t), :] = m.xrecv[par, 1, e, t]
+            A[rows_over(t, -1), :] = m.yrecv[par, 0, 0, t]
+            A[rows_over(t, Y), :] = m.yrecv[par, 1, 0, t]
+            for i in range(4):
+                plane = 1 if i < 2 else X + 2
+                at = -1 if i % 2 == 0 else Y
+                A[rows_of(plane, t, at, 1), :] = m.crecv[par, i, :, tile_of(t)]
+            if r == 0:
+                for side, plane, ring_coef in ((0, 1, 0), (1, X + 2, X + 1)):
+                    B[rows_of(plane, t), :] = m.xrecv[0, side, 2, t]
+                    c = m.xrecv[0, side, 3, t]
+                    C[coef_of(ring_coef, t), :] = c
+                    D[coef_of(ring_coef, t), :] = 2.0 - 6.0 * c
         if r == 0:
-            B[1] = m.xrecv[0, 0, 2]
-            B[X + 2] = m.xrecv[0, 1, 2]
-            C[0] = m.xrecv[0, 0, 3]
-            C[X + 1] = m.xrecv[0, 1, 3]
             m.yold[...] = m.yrecv[0, :, 2]
             m.ycoef[...] = m.yrecv[0, :, 3]
 
         def whole(parts):
             return jnp.concatenate(parts, axis=1)
 
-        def update(field, plane, low_row, high_row, old, coef):
-            n = field[plane]
-            beside = field[plane + 1] + field[plane - 1]
-            beside = beside + jnp.where(row == Y - 1, high_row, pltpu.roll(n, Y - 1, 0))
-            beside = beside + jnp.where(row == 0, low_row, pltpu.roll(n, 1, 0))
-            beside = beside + pltpu.roll(n, W - 1, 1) + pltpu.roll(n, 1, 1)
-            return 2.0 * n - old + coef * (beside - 6.0 * n)
-
-        def side_row(ref, index, x):
-            return whole([ref[(*index, tile, pl.ds(x, 1), slice(None))] for tile in range(T)])
-
-        def first(x, carry):
-            B[x + 2] = update(
-                A,
-                x + 2,
-                side_row(m.yrecv, (par, 0, 0), x),
-                side_row(m.yrecv, (par, 1, 0), x),
-                B[x + 2],
-                C[x + 1],
-            )
+        def beside_of(field, p):
+            def at(plane, shift):
+                return whole([field[rows_of(plane, t, shift), :] for t in range(T)])
+
+            n = at(p, 0)
+            beside = at(p + 1, 0) + at(p - 1, 0)
+            beside = beside + at(p, 1) + at(p, -1)
+            return n, beside + pltpu.roll(n, W - 1, 1) + pltpu.roll(n, 1, 1)
+
+        def update(field, other, p):
+            n, beside = beside_of(field, p)
+            old = whole([other[rows_of(p, t), :] for t in range(T)])
+            c = whole([C[coef_of(p - 1, t), :] for t in range(T)])
+            d = whole([D[coef_of(p - 1, t), :] for t in range(T)])
+            return d * n - old + c * beside
+
+        def first(p, carry):
+            after = update(A, B, p)
+            for t in range(T):
+                B[rows_of(p, t), :] = after[:, tile_of(t)]
             return carry
 
-        lax.fori_loop(0, X, first, 0)
-        for plane, lines in ((1, (0, 1)), (X + 2, (2, 3))):
-            B[plane] = update(
-                A,
-                plane,
-                m.crecv[par, lines[0]],
-                m.crecv[par, lines[1]],
-                B[plane],
-                C[plane - 1],
-            )
+        lax.fori_loop(1, X + 3, first, 0, unroll=2)
         across = lax.broadcasted_iota(jnp.int32, (X, W), 0)
         for side in range(2):
 
@@ -520,8 +547,9 @@
                 - plane_of(m.yold, side)
                 + plane_of(m.ycoef, side) * (beside - 6.0 * n)
             )
-            for tile in range(T):
-                m.yold[side, tile] = value[:, tile * LANES : (tile + 1) * LANES]
+            for t in range(T):
+                m.yold[side, t] = value[:, tile_of(t)]
+                B[rows_over(t, -1 if side == 0 else Y), :] = value[:, tile_of(t)]
         if r == 0:
             sent(range(4), 0, 1)
             sent(range(4), 0, 2)
@@ -530,27 +558,23 @@
         sent(range(4, 8), par, 0)
         final_round = r == STEPS // 2 - 1
 
-        def second(x, carry):
-            after = update(
-                B,
-                x + 2,
-                side_row(m.yold, (0,), x),
-                side_row(m.yold, (1,), x),
-                A[x + 2],
-                C[x + 1],
-            )
+        def second(p, carry):
+            after = update(B, A, p)
             if final_round:
-                out_ref[x] = after[:, 0:Z]
+                out_ref[p - 2] = after[:, 0:Z]
             else:
-                A[x + 2] = after
-                put_rows(0, x, after, range(T), True)
+                for t in range(T):
+                    A[rows_of(p, t), :] = after[:, tile_of(t)]
             return carry
 
-        lax.fori_loop(0, X, second, 0)
+        lax.fori_loop(2, X + 2, second, 0, unroll=2)
         if not final_round:
             put_lines()
             start(range(4, 8), 1 - par, 0)
-            start(range(4), 1 - par, 0)
+            put_planes(2, range(T))
+            start(range(2), 1 - par, 0)
+            put_rows(2, range(T))
+            start(range(2, 4), 1 - par, 0)
         if r == 0:
             load_in.wait()
             load_out.wait()
@@ -565,129 +589,165 @@
         if r == 2:
             m.total[...] = count_finish(2)
 
-    turn(out_ref, 0)
+    turn(out_ref)
     lax.fori_loop(0, slots, pick_targets, 0, unroll=8)
     m.targets[0:slots] = in_order(picked_values(), m.order[...], 2)
     swap(m.targets, 1).start()
     backward(0, m.nrecv[0, gx][0:1, 0:1])
     swap(m.targets, 1).wait()
     backward(1, m.nrecv[0, high * 2 + 1 - core][0:1, 0:1])
+    half = 512
+    places = ((gz, lambda v: device(x=v)), (y, lambda v: device(y=v)))
+
+    def ring(along, piece, relay, fin, send, sems):
+        me, to = places[along]
+        plus, minus, opposed = [lax.rem(me + d, 4) for d in (1, 3, 2)]
+        begin, end = pl.ds(0, 2), pl.ds(2, 2)
+
+        def copy(src, dst, number, peer):
+            return remote(src, dst, sems.at[0, number], sems.at[1, number], to(peer))
+
+        copies = [
+            copy(piece(begin, opposed), relay.at[0], 0, plus),
+            copy(piece(end, opposed), relay.at[1], 1, minus),
+            copy(piece(end, plus), fin.at[0, end], 2, plus),
+            copy(piece(begin, minus), fin.at[1, begin], 3, minus),
+            copy(send.at[0], fin.at[0, begin], 4, plus),
+            copy(send.at[1], fin.at[1, end], 5, minus),
+        ]
+
+        def open_ring():
+            for one in copies[:4]:
+                one.start()
+
+        def pass_on():
+            copies[0].wait_recv()
+            send[0] = relay[0] + piece(begin, plus)[...]
+            copies[4].start()
+            copies[1].wait_recv()
+            send[1] = relay[1] + piece(end, minus)[...]
+            copies[5].start()
+
+        def close_ring():
+            for one in copies[2:]:
+                one.wait_recv()
+            total = piece(pl.ds(0, 4), me)[...] + fin[0] + fin[1]
+            for one in copies:
+                one.wait_send()
+            return total
+
+        return open_ring, pass_on, close_ring
+
+    def piece1(batch, colour):
+        def piece(part, owner):
+            rows = pl.ds(pl.multiple_of(batch * 64 + owner * 16, 8), 16)
+            return m.sums.at[part, rows, pl.ds(colour * half, half)]
+
+        return piece
+
+    def piece2(number):
+        def piece(part, owner):
+            lanes = pl.ds(pl.multiple_of(owner * LANES, LANES), LANES)
+            return m.held1.at[number, part, :, lanes]
+
+        return piece
+
+    def rings_of(batch):
+        one, two = [], []
+        for colour in range(2):
+            q = batch * 2 + colour
+            one.append(
+                ring(
+                    colour,
+                    piece1(batch, colour),
+                    m.relay1.at[q],
+                    m.fin1.at[q],
+                    m.send1.at[q],
+                    m.sems1.at[q],
+                )
+            )
+            two.append(
+                ring(
+                    1 - colour,
+                    piece2(q),
+                    m.relay2.at[q],
+                    m.fin2.at[q],
+                    m.send2.at[q],
+                    m.sems2.at[q],
+                )
+            )
+        return one, two
+
+    batches = [rings_of(batch) for batch in range(2)]
+
+    def run(batch, stage, what, held=None):
+        for colour, one in enumerate(batches[batch][stage]):
+            value = one[what]()
+            if held is not None:
+                held[batch * 2 + colour] = value
+
+    z_me = high * 2 + low
+
+    def z_piece(batch, h, l):
+        rows = pl.ds(pl.multiple_of(l * 8, 8), 8)
+        return m.held2.at[pl.ds(batch * 2, 2), h, rows, :]
+
+    z_peers = []
+    for h, l in z_steps:
+        ph, pw = lax.rem(high + h, 4), lax.rem(low + l, 2)
+        z_peers.append((ph, pw, ph * 2 + pw, device(high=ph, low=pw)))
+
+    def z_copy_out(batch, number):
+        ph, pw, slot, peer = z_peers[number]
+        return remote(
+            z_piece(batch, ph, pw),
+            m.zgot.at[z_me, batch],
+            m.zp_send.at[batch, number],
+            m.zp_recv.at[batch, z_me],
+            peer,
+        )
+
+    def z_start(batch):
+        for number in range(7):
+            z_copy_out(batch, number).start()
+        m.zgot[z_me, batch] = z_piece(batch, high, low)[...]
+
+    def z_finish(batch):
+        for number in range(7):
+            ph, pw, slot, peer = z_peers[number]
+            remote(
+                z_piece(batch, high, low),
+                m.zgot.at[slot, batch],
+                m.zp_send.at[batch, number],
+                m.zp_recv.at[batch, slot],
+                peer,
+            ).wait_recv()
+
     grad_in = matmul(m.normed[...], m.dpre[...], ((0,), (0,)))
+    for h in range(4):
+        m.sums[h, 0:64] = grad_in[h * 64 : (h + 1) * 64]
+    run(0, 0, 0)
     dout = m.dout[...]
     for h in range(4):
         block = pl.multiple_of((h * 2 + core) * LANES, LANES)
         grad_out = matmul(m.act[:, pl.ds(block, LANES)], dout, ((0,), (0,)))
-        m.sums[h, 0:64] = grad_in[h * 64 : (h + 1) * 64]
         m.sums[h, 64:128, 0:512] = grad_out[0:64]
         m.sums[h, 64:128, 512:1024] = grad_out[64:128]
-
-    half = 512
-    places = ((gz, lambda v: device(x=v)), (y, lambda v: device(y=v)))
-
-    def ring(stage, colour, source, rows, relay, fin, send, sems):
-        along = colour if stage == 0 else 1 - colour
-        me, to = places[along]
-        plus, minus, opposed = [lax.rem(me + d, 4) for d in (1, 3, 2)]
-
-        def chunk(owner):
-            return pl.ds(pl.multiple_of(owner * rows, 8), rows)
-
-        begin, end = pl.ds(0, 2), pl.ds(2, 2)
-
-        def piece(part, owner):
-            return source(part, chunk(owner))
-
-        def copy(src, dst, number, peer):
-            return remote(
-                src,
-                dst,
-                sems.at[colour, 0, number],
-                sems.at[colour, 1, number],
-                to(peer),
-            )
-
-        copies = [
-            copy(piece(begin, opposed), relay.at[colour, 0], 0, plus),
-            copy(piece(end, opposed), relay.at[colour, 1], 1, minus),
-            copy(piece(end, plus), fin.at[colour, 0, end], 2, plus),
-            copy(piece(begin, minus), fin.at[colour, 1, begin], 3, minus),
-            copy(send.at[colour, 0], fin.at[colour, 0, begin], 4, plus),
-            copy(send.at[colour, 1], fin.at[colour, 1, end], 5, minus),
-        ]
-
-        def open_ring():
-            for one in copies[:4]:
-                one.start()
-
-        def pass_on():
-            copies[0].wait_recv()
-            send[colour, 0] = relay[colour, 0] + piece(begin, plus)[...]
-            copies[4].start()
-            copies[1].wait_recv()
-            send[colour, 1] = relay[colour, 1] + piece(end, minus)[...]
-            copies[5].start()
-
-        def close_ring():
-            for one in copies[2:]:
-                one.wait_recv()
-            own = piece(pl.ds(0, 4), me)[...]
-            total = own + fin[colour, 0] + fin[colour, 1]
-            for one in copies:
-                one.wait_send()
-            return total
-
-        return open_ring, pass_on, close_ring
-
-    def source1(colour):
-        return lambda part, rows: m.sums.at[part, rows, pl.ds(colour * half, half)]
-
-    def source2(colour):
-        return lambda part, rows: m.held1.at[colour, part, rows, :]
-
-    stage1 = [
-        ring(0, colour, source1(colour), 32, m.relay1, m.fin1, m.send1, m.sems1)
-        for colour in range(2)
-    ]
-    stage2 = [
-        ring(1, colour, source2(colour), 8, m.relay2, m.fin2, m.send2, m.sems2)
-        for colour in range(2)
-    ]
-    for rings, held in ((stage1, m.held1), (stage2, m.held2)):
-        for one in rings:
-            one[0]()
-        for one in rings:
-            one[1]()
-        for colour, one in enumerate(rings):
-            held[colour] = one[2]()
-
-    z_me = high * 2 + low
-    quarter = half // 2
-
-    def z_piece(h, l):
-        return m.held2.at[:, h, :, pl.ds(pl.multiple_of(l * quarter, quarter), quarter)]
-
-    z_copies = []
-    for number, (h, l) in enumerate(z_steps):
-        ph, pw = lax.rem(high + h, 4), lax.rem(low + l, 2)
-        peer = device(high=ph, low=pw)
-        one = remote(
-            z_piece(ph, pw),
-            m.zgot.at[z_me],
-            m.zp_send.at[number],
-            m.zp_recv.at[z_me],
-            peer,
-        )
-        one.start()
-        z_copies.append((one, ph * 2 + pw, peer))
-    m.zgot[z_me] = z_piece(high, low)[...]
-    for one, slot, peer in z_copies:
-        remote(
-            z_piece(high, low),
-            m.zgot.at[slot],
-            m.zp_send.at[0],
-            m.zp_recv.at[slot],
-            peer,
-        ).wait_recv()
+    run(1, 0, 0)
+    run(0, 0, 1)
+    run(1, 0, 1)
+    run(0, 0, 2, m.held1)
+    run(0, 1, 0)
+    run(1, 0, 2, m.held1)
+    run(1, 1, 0)
+    run(0, 1, 1)
+    run(1, 1, 1)
+    run(0, 1, 2, m.held2)
+    z_start(0)
+    run(1, 1, 2, m.held2)
+    z_start(1)
+    z_finish(0)
+    z_finish(1)
     total = m.zgot[0]
     for slot in range(1, 8):
         total = total + m.zgot[slot]
@@ -706,8 +766,9 @@
         )
         one.start()
         g_copies.append((one, (px * 4 + py) * 2 + pw, peer))
-    for one, slot, peer in z_copies:
-        one.wait_send()
+    for batch in range(2):
+        for number in range(7):
+            z_copy_out(batch, number).wait_send()
     for one, slot, peer in g_copies:
         remote(
             m.gathered.at[slot],
@@ -740,11 +801,14 @@
         return pltpu.VMEM(shape, BF16)
 
     scratch = dict(
-        A=f32(X + 4, Y, W),
-        B=f32(X + 4, Y, W),
-        C=f32(X + 2, Y, W),
-        xsend=f32(2, 4, Y, W),
-        xrecv=f32(2, 2, 4, Y, W),
+        A=f32(2 * PAD + (X + 4) * T * R, LANES),
+        B=f32(2 * PAD + (X + 4) * T * R, LANES),
+        C=f32((X + 2) * T * Y, LANES),
+        D=f32((X + 2) * T * Y, LANES),
+        now=f32(X, Y, Z),
+        prev=f32(X, Y, Z),
+        xsend=f32(2, 4, T, Y, LANES),
+        xrecv=f32(2, 2, 4, T, Y, LANES),
         ysend=f32(2, 4, T, X, LANES),
         yrecv=f32(2, 2, 4, T, X, LANES),
         yold=f32(2, T, X, LANES),
@@ -773,16 +837,16 @@
         dout=b16(2 * slots, wide),
         dpre=b16(2 * slots, hidden),
         sums=f32(4, 128, 1024),
-        relay1=f32(2, 2, 2, 32, 512),
-        fin1=f32(2, 2, 4, 32, 512),
-        send1=f32(2, 2, 2, 32, 512),
-        held1=f32(2, 4, 32, 512),
-        relay2=f32(2, 2, 2, 8, 512),
-        fin2=f32(2, 2, 4, 8, 512),
-        send2=f32(2, 2, 2, 8, 512),
-        held2=f32(2, 4, 8, 512),
-        zgot=f32(8, 2, 8, 256),
-        gathered=f32(32, 2, 8, 256),
+        relay1=f32(4, 2, 2, 16, 512),
+        fin1=f32(4, 2, 4, 16, 512),
+        send1=f32(4, 2, 2, 16, 512),
+        held1=f32(4, 4, 16, 512),
+        relay2=f32(4, 2, 2, 16, LANES),
+        fin2=f32(4, 2, 4, 16, LANES),
+        send2=f32(4, 2, 2, 16, LANES),
+        held2=f32(4, 4, 16, LANES),
+        zgot=f32(8, 2, 2, 8, LANES),
+        gathered=f32(32, 2, 2, 8, LANES),
         load=dma((5,)),
         z_sem=dma((2, 2)),
         f_send=dma((12,)),
@@ -791,10 +855,10 @@
         n_recv=dma((3, most)),
         p_send=dma((2,)),
         p_recv=dma((2,)),
-        sems1=dma((2, 2, 6)),
-        sems2=dma((2, 2, 6)),
-        zp_send=dma((7,)),
-        zp_recv=dma((8,)),
+        sems1=dma((4, 2, 6)),
+        sems2=dma((4, 2, 6)),
+        zp_send=dma((2, 7)),
+        zp_recv=dma((2, 8)),
         g_send=dma((31,)),
         g_recv=dma((32,)),
     )
@@ -803,7 +867,7 @@
         name="step",
         out_shape=(
             jax.ShapeDtypeStruct((X, Y, Z), F32),
-            jax.ShapeDtypeStruct((32, 2, 8, 256), F32),
+            jax.ShapeDtypeStruct((32, 2, 2, 8, LANES), F32),
         ),
         in_specs=[hbm, hbm, hbm, smem, smem, smem, hbm, hbm],
         out_specs=(vmem, vmem),
@@ -821,15 +885,13 @@
     for slot in range(32):
         ix, iy, il = slot // 8, slot // 2 % 4, slot % 2
         for colour in range(2):
-            row = ix * 32 + iy * 8 if colour == 0 else iy * 32 + ix * 8
-            at = colour * 512 + il * 256
-            value = sum_ref[slot, colour]
-            if row < 64:
-                in_ref[row : row + 8, at : at + 256] = value
-            else:
-                top = row - 64 + (64 if at >= 512 else 0)
-                left = at % 512
-                out_ref[top : top + 8, left : left + 256] = value
+            one, two = (ix, iy) if colour == 0 else (iy, ix)
+            top = one * 16 + il * 8
+            at = two * LANES
+            left = colour * 512 + at
+            low = colour * 64 + top
+            in_ref[top : top + 8, left : left + LANES] = sum_ref[slot, 0, colour]
+            out_ref[low : low + 8, at : at + LANES] = sum_ref[slot, 1, colour]
 
 
 def place(final, sums):

time: 88.5 us -> 83.8 us (0.947)
  Pallas kernels: 87.2 us -> 82.5 us
    pallas_call x1, Pallas kernels: 86.2 us -> 81.5 us  [step(): pl.pallas_call(functools.partial(step_kernel, tuple(scratch), sizes), nam...]
where the time goes in v4:
time: 83.8 us; the launch traced here: 83.7 us
  Pallas kernels  82.5 us (98%)
  between operations  1.29 us (2%)
    pallas_call x1, Pallas kernels, step(): pl.pallas_call(functools.partial(step_kernel, tuple(scratch), sizes), nam...  81.5 us

profile of v4, /device:TPU:8, one launch (start us, length us, event | category | flops | bytes accessed | tf_op | source)
XLA Modules:
  0.0 83.7 jit_solution(3800987390701556749)
XLA Ops:
  1.3 81.5 %step.1 = (f32[16,24,256]{2,1,0:T(8,128)S(1)}, f32[32,2,2,8,128]{4,3,2,1,0:T(8,128)S(1)}) custom-call(f32[16,24,256]{2,1,0:T(8,128)} %prev_hbm.1, f32[16,24,256]{2,1,0:T(8,128)} %now_hbm.1, s32[16,24,256]{2,1,0:T(8,128)} %mat_hbm.1, f32[8]{0:T(128)} %tab_ref.1, s32[1]{0:T(128)} %bitcast.2.cnt_ref, s32[128]{0:T(128)} %bitcast.3, bf16[512,1024]{1,0:T(8,128)(2,1)} %win_hbm.1, ...), custom_call_target="tpu_custom_call" | custom-call | tf_op jit(solution)/shard_map/step/pallas_call | solution.py:865
  82.8 1.0 %place.1 = (f32[16,24,256]{2,1,0:T(8,128)}, f32[64,1024]{1,0:T(8,128)}, f32[128,512]{1,0:T(8,128)}) custom-call(f32[16,24,256]{2,1,0:T(8,128)S(1)} %get-tuple-element.5.final_ref, f32[32,2,2,8,128]{4,3,2,1,0:T(8,128)S(1)} %get-tuple-element.6.sum_ref), custom_call_target="tpu_custom_call" | custom-call | tf_op jit(solution)/shard_map/place/pallas_call | solution.py:899

commit v5 on v4

--- a/solution.py
+++ b/solution.py
@@ -148,34 +148,83 @@
     load_in.start()
     load_out.start()
 
-    m.xrecv[...] = jnp.zeros(m.xrecv.shape, F32)
-    m.yrecv[...] = jnp.zeros(m.yrecv.shape, F32)
-    m.zrecv[...] = jnp.zeros(m.zrecv.shape, F32)
-    m.crecv[...] = jnp.zeros(m.crecv.shape, F32)
+    def clear(missing, ref, *index):
+        @pl.when(missing)
+        def _():
+            for par in range(2):
+                ref[(par, *index)] = jnp.zeros(ref.shape[1 + len(index) :], F32)
+
+    ends = ((gx == 0, gx == nx - 1), (gy == 0, gy == ny - 1))
+    for side in range(2):
+        clear(ends[0][side], m.xrecv, side)
+        clear(ends[1][side], m.yrecv, side)
+        for other in range(2):
+            clear(
+                jnp.logical_or(ends[0][side], ends[1][other]),
+                m.crecv,
+                side * 2 + other,
+            )
+
+    @pl.when(gz == 0)
+    def _():
+        m.zrecv[0] = jnp.zeros(m.zrecv.shape[1:], F32)
+
+    @pl.when(gz == nz - 1)
+    def _():
+        m.zrecv[1] = jnp.zeros(m.zrecv.shape[1:], F32)
+
     for place in reached:
         signal(barrier, place)
 
     lane = lax.broadcasted_iota(jnp.int32, (Y, LANES), 1)
-    def put_rows(entries, tiles):
+    def pack_edge(values):
+        at = lax.broadcasted_iota(jnp.int32, values[0].shape, 1)
+        group = lax.shift_right_logical(jnp.bitwise_and(at + 8, LANES - 1), 4)
+        packed = values[0]
+        for e, value in enumerate(values[1:], 1):
+            packed = jnp.where(group == e, pltpu.roll(value, 16 * e, 1), packed)
+        return packed
+
+    def open_edge(packed, e, masked=False):
+        value = pltpu.roll(packed, LANES - 16 * e, 1) if e else packed
+        if masked:
+            at = lax.broadcasted_iota(jnp.int32, value.shape, 1)
+            value = jnp.where((at < 8) | (at >= LANES - 8), value, 0.0)
+        return value
+
+    def face_tiles(ref, index, e, masked=False):
+        tiles = [ref[(*index, 1 + 2 * e + t)] for t in range(2)]
+        return tiles + [open_edge(ref[(*index, 0)], e, masked)]
+
+    def put_face(ref, side, sources, main, edge):
+        if main:
+            for e, source in enumerate(sources):
+                for t in range(2):
+                    ref[side, 1 + 2 * e + t] = source(t)
+        if edge:
+            ref[side, 0] = pack_edge([source(2) for source in sources])
+
+    def put_rows(entries, main, edge):
         for side, at, second in ((0, 0, 1), (1, Y - 1, Y - 2)):
-            for t in tiles:
-                m.ysend[side, 0, t] = A[rows_over(t, at), :]
-                m.ysend[side, 1, t] = A[rows_over(t, second), :]
-                if entries > 2:
-                    m.ysend[side, 2, t] = B[rows_over(t, at), :]
-                    m.ysend[side, 3, t] = C[coef_over(t, at), :]
-
-    def put_planes(entries, tiles):
+            sources = [
+                lambda t, at=at: A[rows_over(t, at), :],
+                lambda t, second=second: A[rows_over(t, second), :],
+                lambda t, at=at: B[rows_over(t, at), :],
+                lambda t, at=at: C[coef_over(t, at), :],
+            ][:entries]
+            put_face(m.ysend, side, sources, main, edge)
+
+    def put_planes(entries, main, edge):
         for side, planes in enumerate(((2, 3, 2, 1), (X, X + 1, X + 1, X))):
-            for t in tiles:
-                m.xsend[side, 0, t] = A[rows_of(planes[0], t), :]
-                m.xsend[side, 1, t] = A[rows_of(planes[1], t), :]
-                if entries > 2:
-                    m.xsend[side, 2, t] = B[rows_of(planes[2], t), :]
-                    m.xsend[side, 3, t] = C[coef_of(planes[3], t), :]
+            sources = [
+                lambda t, p=planes[0]: A[rows_of(p, t), :],
+                lambda t, p=planes[1]: A[rows_of(p, t), :],
+                lambda t, p=planes[2]: B[rows_of(p, t), :],
+                lambda t, p=planes[3]: C[coef_of(p, t), :],
+            ][:entries]
+            put_face(m.xsend, side, sources, main, edge)
 
     inner_tiles = range(Z // LANES)
-    last_tile = range(Z // LANES, T)
 
     for one in loads:
         one.wait()
@@ -206,8 +255,8 @@
         m.zsend[0, i] = ups[i]
         m.zsend[1, i] = downs[i]
 
-    put_planes(4, inner_tiles)
-    put_rows(4, inner_tiles)
+    put_planes(4, True, False)
+    put_rows(4, True, False)
     m.nsend[0] = jnp.full((8, LANES), cnt_ref[0].astype(F32))
 
     pl.semaphore_wait(barrier, len(reached))
@@ -249,23 +298,12 @@
     opposite = (1, 0, 3, 2, 7, 6, 5, 4)
 
     def face(d, par, form):
-        if d < 2:
-            if form == 0:
-                src = m.xsend.at[d, 0:2]
-                dst = m.xrecv.at[par, 1 - d, 0:2]
-            else:
-                tiles = pl.ds(0, T - 1) if form == 1 else pl.ds(T - 1, 1)
-                src = m.xsend.at[d, :, tiles]
-                dst = m.xrecv.at[par, 1 - d, :, tiles]
-        elif d < 4:
-            side = d - 2
-            if form == 0:
-                src = m.ysend.at[side, 0:2]
-                dst = m.yrecv.at[par, 1 - side, 0:2]
-            else:
-                tiles = pl.ds(0, T - 1) if form == 1 else pl.ds(T - 1, 1)
-                src = m.ysend.at[side, :, tiles]
-                dst = m.yrecv.at[par, 1 - side, :, tiles]
+        if d < 4:
+            side = d % 2
+            send, got = (m.xsend, m.xrecv) if d < 2 else (m.ysend, m.yrecv)
+            tiles = (pl.ds(0, 5), pl.ds(1, 8), pl.ds(0, 1))[form]
+            src = send.at[side, tiles]
+            dst = got.at[par, 1 - side, tiles]
         else:
             src = m.csend.at[d - 4]
             dst = m.crecv.at[par, 7 - d]
@@ -337,35 +375,34 @@
                 ]
         for half in range(Z // LANES):
             for tile in range(tiles):
-                m.turned[tile, half * LANES : (half + 1) * LANES, :] = m.rows[
+                at = tile * Z + half * LANES
+                m.turned[at : at + LANES, :] = m.rows[
                     half, tile * LANES : (tile + 1) * LANES, :
                 ].T
 
-    def pick_one(s, tile, k, by):
-        first = m.turned[tile, pl.ds(k, 8), :]
-        second = m.turned[tile + 1, pl.ds(k, 8), :]
-        back = lax.rem(LANES - by, LANES)
+    def pick_one(s, first_row, keep):
+        first = m.turned[pl.ds(first_row, 8), :]
+        second = m.turned[pl.ds(first_row + Z, 8), :]
+        back = jnp.bitwise_and(keep, LANES - 1)
         m.picked[pl.ds(pl.multiple_of(s * 8, 8), 8), :] = jnp.where(
-            narrow < LANES - by,
-            pltpu.roll(first, back, 1),
-            pltpu.roll(second, back, 1),
+            narrow < keep, pltpu.roll(first, back, 1), pltpu.roll(second, back, 1)
         )
 
     def pick_inputs(s, carry):
         anchor = anchor_ref[s]
         i = anchor // (Y * Z)
-        j = lax.rem(anchor // Z, Y)
-        k = lax.rem(anchor, Z)
+        rest = anchor - i * (Y * Z)
+        j = rest // Z
         shift = j * X + i
-        tile, by = shift // LANES, lax.rem(shift, LANES)
-        m.where[0, s] = tile
-        m.where[1, s] = k
-        m.where[2, s] = by
-        pick_one(s, tile, k, by)
+        first_row = (shift // LANES) * Z + (rest - j * Z)
+        keep = LANES - jnp.bitwise_and(shift, LANES - 1)
+        m.where[0, s] = first_row
+        m.where[1, s] = keep
+        pick_one(s, first_row, keep)
         return carry
 
     def pick_targets(s, carry):
-        pick_one(s, m.where[0, s], m.where[1, s], m.where[2, s])
+        pick_one(s, m.where[0, s], m.where[1, s])
         return carry
 
     def picked_values():
@@ -382,7 +419,7 @@
             partner,
         )
 
-    m.turned[tiles] = jnp.zeros((Z, LANES), F32)
+    m.turned[tiles * Z : (tiles + 1) * Z, :] = jnp.zeros((Z, LANES), F32)
     turn(m.now)
 
     @pl.when(gz < nz - 1)
@@ -418,8 +455,8 @@
             for t in range(T):
                 m.csend[i, :, tile_of(t)] = A[rows_of(plane, t, at, 1), :]
 
-    put_planes(4, last_tile)
-    put_rows(4, last_tile)
+    put_planes(4, False, True)
+    put_rows(4, False, True)
     put_lines()
     start(range(4, 8), 0, 0)
     start(range(4), 0, 2)
@@ -478,25 +515,30 @@
         else:
             came(range(4), par, 0)
         came(range(4, 8), par, 0)
+        for side in range(2):
+            for e in range(2):
+                plane = e + side * (X + 2)
+                for t, value in enumerate(face_tiles(m.xrecv, (par, side), e)):
+                    A[rows_of(plane, t), :] = value
+            for t, value in enumerate(face_tiles(m.yrecv, (par, side), 0)):
+                A[rows_over(t, -1 if side == 0 else Y), :] = value
         for t in range(T):
-            for e in range(2):
-                A[rows_of(e, t), :] = m.xrecv[par, 0, e, t]
-                A[rows_of(X + 2 + e, t), :] = m.xrecv[par, 1, e, t]
-            A[rows_over(t, -1), :] = m.yrecv[par, 0, 0, t]
-            A[rows_over(t, Y), :] = m.yrecv[par, 1, 0, t]
             for i in range(4):
                 plane = 1 if i < 2 else X + 2
                 at = -1 if i % 2 == 0 else Y
                 A[rows_of(plane, t, at, 1), :] = m.crecv[par, i, :, tile_of(t)]
-            if r == 0:
-                for side, plane, ring_coef in ((0, 1, 0), (1, X + 2, X + 1)):
-                    B[rows_of(plane, t), :] = m.xrecv[0, side, 2, t]
-                    c = m.xrecv[0, side, 3, t]
-                    C[coef_of(ring_coef, t), :] = c
-                    D[coef_of(ring_coef, t), :] = 2.0 - 6.0 * c
         if r == 0:
-            m.yold[...] = m.yrecv[0, :, 2]
-            m.ycoef[...] = m.yrecv[0, :, 3]
+            for side, plane, ring_coef in ((0, 1, 0), (1, X + 2, X + 1)):
+                olds = face_tiles(m.xrecv, (0, side), 2)
+                coefs = face_tiles(m.xrecv, (0, side), 3, True)
+                side_olds = face_tiles(m.yrecv, (0, side), 2)
+                side_coefs = face_tiles(m.yrecv, (0, side), 3, True)
+                for t in range(T):
+                    B[rows_of(plane, t), :] = olds[t]
+                    C[coef_of(ring_coef, t), :] = coefs[t]
+                    D[coef_of(ring_coef, t), :] = 2.0 - 6.0 * coefs[t]
+                    m.yold[side, t] = side_olds[t]
+                    m.ycoef[side, t] = side_coefs[t]
 
         def whole(parts):
             return jnp.concatenate(parts, axis=1)
@@ -530,9 +572,9 @@
             def plane_of(ref, *index):
                 return whole([ref[(*index, tile)] for tile in range(T)])
 
-            n = plane_of(m.yrecv, par, side, 0)
-            outer = plane_of(m.yrecv, par, side, 1)
-            inner = plane_of(m.ysend, side, 0)
+            n = whole(face_tiles(m.yrecv, (par, side), 0))
+            outer = whole(face_tiles(m.yrecv, (par, side), 1))
+            inner = whole([A[rows_over(t, side * (Y - 1)), :] for t in range(T)])
             plus, minus = (inner, outer) if side == 0 else (outer, inner)
             beside = jnp.where(
                 across == X - 1, m.crecv[par, 2 + side], pltpu.roll(n, X - 1, 0)
@@ -571,9 +613,9 @@
         if not final_round:
             put_lines()
             start(range(4, 8), 1 - par, 0)
-            put_planes(2, range(T))
+            put_planes(2, True, True)
             start(range(2), 1 - par, 0)
-            put_rows(2, range(T))
+            put_rows(2, True, True)
             start(range(2, 4), 1 - par, 0)
         if r == 0:
             load_in.wait()
@@ -590,7 +632,7 @@
             m.total[...] = count_finish(2)
 
     turn(out_ref)
-    lax.fori_loop(0, slots, pick_targets, 0, unroll=8)
+    lax.fori_loop(0, slots, pick_targets, 0, unroll=16)
     m.targets[0:slots] = in_order(picked_values(), m.order[...], 2)
     swap(m.targets, 1).start()
     backward(0, m.nrecv[0, gx][0:1, 0:1])
@@ -746,40 +788,39 @@
     z_start(0)
     run(1, 1, 2, m.held2)
     z_start(1)
-    z_finish(0)
-    z_finish(1)
-    total = m.zgot[0]
-    for slot in range(1, 8):
-        total = total + m.zgot[slot]
     g_me = (gz * 4 + y) * 2 + low
-    m.gathered[g_me] = total
-    g_copies = []
-    for number, (i, j, l) in enumerate(g_steps):
+    g_peers = []
+    for i, j, l in g_steps:
         px, py, pw = lax.rem(gz + i, 4), lax.rem(y + j, 4), lax.rem(low + l, 2)
-        peer = device(x=px, y=py, low=pw)
-        one = remote(
-            m.gathered.at[g_me],
-            m.gathered.at[g_me],
-            m.g_send.at[number],
-            m.g_recv.at[g_me],
-            peer,
+        g_peers.append(((px * 4 + py) * 2 + pw, device(x=px, y=py, low=pw)))
+
+    def g_copy(batch, number, slot):
+        return remote(
+            m.gathered.at[slot, batch],
+            m.gathered.at[slot, batch],
+            m.g_send.at[batch, number],
+            m.g_recv.at[batch, slot],
+            g_peers[number][1],
         )
-        one.start()
-        g_copies.append((one, (px * 4 + py) * 2 + pw, peer))
+
+    for batch in range(2):
+        z_finish(batch)
+        total = m.zgot[0, batch]
+        for slot in range(1, 8):
+            total = total + m.zgot[slot, batch]
+        m.gathered[g_me, batch] = total
+        for number in range(31):
+            g_copy(batch, number, g_me).start()
     for batch in range(2):
         for number in range(7):
             z_copy_out(batch, number).wait_send()
-    for one, slot, peer in g_copies:
-        remote(
-            m.gathered.at[slot],
-            m.gathered.at[slot],
-            m.g_send.at[0],
-            m.g_recv.at[slot],
-            peer,
-        ).wait_recv()
+    for batch in range(2):
+        for number in range(31):
+            g_copy(batch, number, g_peers[number][0]).wait_recv()
     sum_ref[...] = m.gathered[...]
-    for one, slot, peer in g_copies:
-        one.wait_send()
+    for batch in range(2):
+        for number in range(31):
+            g_copy(batch, number, g_me).wait_send()
 
 
 def step(prev, now, material, table, used, anchors, w_in, w_out, sizes):
@@ -807,10 +848,10 @@
         D=f32((X + 2) * T * Y, LANES),
         now=f32(X, Y, Z),
         prev=f32(X, Y, Z),
-        xsend=f32(2, 4, T, Y, LANES),
-        xrecv=f32(2, 2, 4, T, Y, LANES),
-        ysend=f32(2, 4, T, X, LANES),
-        yrecv=f32(2, 2, 4, T, X, LANES),
+        xsend=f32(2, 9, Y, LANES),
+        xrecv=f32(2, 2, 9, Y, LANES),
+        ysend=f32(2, 9, X, LANES),
+        yrecv=f32(2, 2, 9, X, LANES),
         yold=f32(2, T, X, LANES),
         ycoef=f32(2, T, X, LANES),
         csend=f32(4, 1, W),
@@ -821,10 +862,10 @@
         nrecv=f32(3, most, 8, LANES),
         total=f32(8, LANES),
         rows=f32(Z // LANES, X * Y, LANES),
-        turned=f32(X * Y // LANES + 1, Z, LANES),
+        turned=f32((X * Y // LANES + 1) * Z, LANES),
         picked=f32(8 * slots, LANES),
         mat=pltpu.VMEM((X, Y, Z), jnp.int32),
-        where=pltpu.SMEM((3, slots), jnp.int32),
+        where=pltpu.SMEM((2, slots), jnp.int32),
         order=b16(8 * LANES, wide),
         w_in=b16(wide, hidden),
         w_out=b16(hidden, wide),
@@ -859,8 +900,8 @@
         sems2=dma((4, 2, 6)),
         zp_send=dma((2, 7)),
         zp_recv=dma((2, 8)),
-        g_send=dma((31,)),
-        g_recv=dma((32,)),
+        g_send=dma((2, 31)),
+        g_recv=dma((2, 32)),
     )
     return pl.pallas_call(
         functools.partial(step_kernel, tuple(scratch), sizes),

time: 83.8 us -> 80.8 us (0.964)
  Pallas kernels: 82.5 us -> 79.4 us
    pallas_call x1, Pallas kernels: 81.5 us -> 78.4 us  [step(): pl.pallas_call(functools.partial(step_kernel, tuple(scratch), sizes), nam...]
where the time goes in v5:
time: 80.8 us; the launch traced here: 80.7 us
  Pallas kernels  79.4 us (98%)
  between operations  1.29 us (2%)
    pallas_call x1, Pallas kernels, step(): pl.pallas_call(functools.partial(step_kernel, tuple(scratch), sizes), nam...  78.4 us

profile of v5, /device:TPU:8, one launch (start us, length us, event | category | flops | bytes accessed | tf_op | source)
XLA Modules:
  0.0 80.7 jit_solution(14833099146028692056)
XLA Ops:
  1.3 78.4 %step.1 = (f32[16,24,256]{2,1,0:T(8,128)S(1)}, f32[32,2,2,8,128]{4,3,2,1,0:T(8,128)S(1)}) custom-call(f32[16,24,256]{2,1,0:T(8,128)} %prev_hbm.1, f32[16,24,256]{2,1,0:T(8,128)} %now_hbm.1, s32[16,24,256]{2,1,0:T(8,128)} %mat_hbm.1, f32[8]{0:T(128)} %tab_ref.1, s32[1]{0:T(128)} %bitcast.2.cnt_ref, s32[128]{0:T(128)} %bitcast.3, bf16[512,1024]{1,0:T(8,128)(2,1)} %win_hbm.1, ...), custom_call_target="tpu_custom_call" | custom-call | tf_op jit(solution)/shard_map/step/pallas_call | solution.py:906
  79.7 1.0 %place.1 = (f32[16,24,256]{2,1,0:T(8,128)}, f32[64,1024]{1,0:T(8,128)}, f32[128,512]{1,0:T(8,128)}) custom-call(f32[16,24,256]{2,1,0:T(8,128)S(1)} %get-tuple-element.5.final_ref, f32[32,2,2,8,128]{4,3,2,1,0:T(8,128)S(1)} %get-tuple-element.6.sum_ref), custom_call_target="tpu_custom_call" | custom-call | tf_op jit(solution)/shard_map/place/pallas_call | solution.py:940

commit v6 on v5

--- a/solution.py
+++ b/solution.py
@@ -364,6 +364,68 @@
 
     count_start(0)
 
+    def whole(parts):
+        return jnp.concatenate(parts, axis=1)
+
+    def beside_of(field, p):
+        def at(plane, shift):
+            return whole([field[rows_of(plane, t, shift), :] for t in range(T)])
+
+        n = at(p, 0)
+        beside = at(p + 1, 0) + at(p - 1, 0)
+        beside = beside + at(p, 1) + at(p, -1)
+        return n, beside + pltpu.roll(n, W - 1, 1) + pltpu.roll(n, 1, 1)
+
+    def update(field, other, p):
+        n, beside = beside_of(field, p)
+        old = whole([other[rows_of(p, t), :] for t in range(T)])
+        c = whole([C[coef_of(p - 1, t), :] for t in range(T)])
+        d = whole([D[coef_of(p - 1, t), :] for t in range(T)])
+        return d * n - old + c * beside
+
+    across = lax.broadcasted_iota(jnp.int32, (X, W), 0)
+
+    def side_update(n, plus, minus, ends, old, c, d):
+        beside = jnp.where(across == X - 1, ends[1], pltpu.roll(n, X - 1, 0))
+        beside = beside + jnp.where(across == 0, ends[0], pltpu.roll(n, 1, 0))
+        beside = beside + plus + minus
+        beside = beside + pltpu.roll(n, W - 1, 1) + pltpu.roll(n, 1, 1)
+        return d * n - old + c * beside
+
+    def row_update(field, old, at):
+        def row(shift):
+            return whole([field[rows_over(t, at + shift), :] for t in range(T)])
+
+        ends = [
+            whole([field[rows_of(p, t, at, 1), :] for t in range(T)])
+            for p in (1, X + 2)
+        ]
+        c = whole([C[coef_over(t, at), :] for t in range(T)])
+        d = whole([D[coef_over(t, at), :] for t in range(T)])
+        return side_update(row(0), row(1), row(-1), ends, old, c, d)
+
+    def first(p, carry=0):
+        after = update(A, B, p)
+        for t in range(T):
+            B[rows_of(p, t), :] = after[:, tile_of(t)]
+        return carry
+
+    def second(p, carry=0):
+        after = update(B, A, p)
+        for t in range(T):
+            A[rows_of(p, t), :] = after[:, tile_of(t)]
+        return carry
+
+    def last(p, carry):
+        out_ref[p - 2] = update(B, A, p)[:, 0:Z]
+        return carry
+
+    def early():
+        for side in range(2):
+            for t in range(T):
+                m.held_rows[side, t] = B[rows_over(t, side * (Y - 1)), :]
+        lax.fori_loop(3, X + 1, first, 0, unroll=2)
+
     tiles = X * Y // LANES
     narrow = lax.broadcasted_iota(jnp.int32, (8, LANES), 1)
 
@@ -460,6 +522,7 @@
     put_lines()
     start(range(4, 8), 0, 0)
     start(range(4), 0, 2)
+    early()
 
     lax.fori_loop(0, slots, pick_inputs, 0, unroll=8)
     at = lax.broadcasted_iota(jnp.int32, (8 * LANES, wide), 0)
@@ -540,33 +603,14 @@
                     m.yold[side, t] = side_olds[t]
                     m.ycoef[side, t] = side_coefs[t]
 
-        def whole(parts):
-            return jnp.concatenate(parts, axis=1)
-
-        def beside_of(field, p):
-            def at(plane, shift):
-                return whole([field[rows_of(plane, t, shift), :] for t in range(T)])
-
-            n = at(p, 0)
-            beside = at(p + 1, 0) + at(p - 1, 0)
-            beside = beside + at(p, 1) + at(p, -1)
-            return n, beside + pltpu.roll(n, W - 1, 1) + pltpu.roll(n, 1, 1)
-
-        def update(field, other, p):
-            n, beside = beside_of(field, p)
-            old = whole([other[rows_of(p, t), :] for t in range(T)])
-            c = whole([C[coef_of(p - 1, t), :] for t in range(T)])
-            d = whole([D[coef_of(p - 1, t), :] for t in range(T)])
-            return d * n - old + c * beside
-
-        def first(p, carry):
-            after = update(A, B, p)
+        for p in (1, 2, X + 1, X + 2):
+            first(p)
+        for side in range(2):
+            at = side * (Y - 1)
+            old = whole([m.held_rows[side, t] for t in range(T)])
+            value = row_update(A, old, at)
             for t in range(T):
-                B[rows_of(p, t), :] = after[:, tile_of(t)]
-            return carry
-
-        lax.fori_loop(1, X + 3, first, 0, unroll=2)
-        across = lax.broadcasted_iota(jnp.int32, (X, W), 0)
+                B[rows_over(t, at), :] = value[:, tile_of(t)]
         for side in range(2):
 
             def plane_of(ref, *index):
@@ -576,18 +620,15 @@
             outer = whole(face_tiles(m.yrecv, (par, side), 1))
             inner = whole([A[rows_over(t, side * (Y - 1)), :] for t in range(T)])
             plus, minus = (inner, outer) if side == 0 else (outer, inner)
-            beside = jnp.where(
-                across == X - 1, m.crecv[par, 2 + side], pltpu.roll(n, X - 1, 0)
-            )
-            beside = beside + jnp.where(
-                across == 0, m.crecv[par, side], pltpu.roll(n, 1, 0)
-            )
-            beside = beside + plus + minus
-            beside = beside + pltpu.roll(n, W - 1, 1) + pltpu.roll(n, 1, 1)
-            value = (
-                2.0 * n
-                - plane_of(m.yold, side)
-                + plane_of(m.ycoef, side) * (beside - 6.0 * n)
+            c = plane_of(m.ycoef, side)
+            value = side_update(
+                n,
+                plus,
+                minus,
+                (m.crecv[par, side], m.crecv[par, 2 + side]),
+                plane_of(m.yold, side),
+                c,
+                2.0 - 6.0 * c,
             )
             for t in range(T):
                 m.yold[side, t] = value[:, tile_of(t)]
@@ -600,23 +641,25 @@
         sent(range(4, 8), par, 0)
         final_round = r == STEPS // 2 - 1
 
-        def second(p, carry):
-            after = update(B, A, p)
-            if final_round:
-                out_ref[p - 2] = after[:, 0:Z]
-            else:
-                for t in range(T):
-                    A[rows_of(p, t), :] = after[:, tile_of(t)]
-            return carry
-
-        lax.fori_loop(2, X + 2, second, 0, unroll=2)
-        if not final_round:
+        if final_round:
+            lax.fori_loop(2, X + 2, last, 0, unroll=2)
+        else:
+            for side, rows in ((0, (0, 1)), (1, (Y - 1, Y - 2))):
+                values = []
+                for at in rows:
+                    old = whole([A[rows_over(t, at), :] for t in range(T)])
+                    values.append(row_update(B, old, at))
+                sources = [lambda t, v=v: v[:, tile_of(t)] for v in values]
+                put_face(m.ysend, side, sources, True, True)
+                start((2 + side,), 1 - par, 0)
+            for p in (2, 3, X, X + 1):
+                second(p)
             put_lines()
             start(range(4, 8), 1 - par, 0)
             put_planes(2, True, True)
             start(range(2), 1 - par, 0)
-            put_rows(2, True, True)
-            start(range(2, 4), 1 - par, 0)
+            lax.fori_loop(4, X, second, 0, unroll=2)
+            early()
         if r == 0:
             load_in.wait()
             load_out.wait()
@@ -854,6 +897,7 @@
         yrecv=f32(2, 2, 9, X, LANES),
         yold=f32(2, T, X, LANES),
         ycoef=f32(2, T, X, LANES),
+        held_rows=f32(2, T, X, LANES),
         csend=f32(4, 1, W),
         crecv=f32(2, 4, 1, W),
         zsend=f32(2, 3, Y, LANES),

time: 80.8 us -> 77.6 us (0.960)
  Pallas kernels: 79.4 us -> 75.9 us
    pallas_call x1, Pallas kernels: 78.4 us -> 74.9 us  [step(): pl.pallas_call(functools.partial(step_kernel, tuple(scratch), sizes), nam...]
where the time goes in v6:
time: 77.6 us; the launch traced here: 77.2 us
  Pallas kernels  75.9 us (98%)
  between operations  1.29 us (2%)
    pallas_call x1, Pallas kernels, step(): pl.pallas_call(functools.partial(step_kernel, tuple(scratch), sizes), nam...  74.9 us

profile of v6, /device:TPU:8, one launch (start us, length us, event | category | flops | bytes accessed | tf_op | source)
XLA Modules:
  0.0 77.2 jit_solution(17838017701956322169)
XLA Ops:
  1.3 74.9 %step.1 = (f32[16,24,256]{2,1,0:T(8,128)S(1)}, f32[32,2,2,8,128]{4,3,2,1,0:T(8,128)S(1)}) custom-call(f32[16,24,256]{2,1,0:T(8,128)} %prev_hbm.1, f32[16,24,256]{2,1,0:T(8,128)} %now_hbm.1, s32[16,24,256]{2,1,0:T(8,128)} %mat_hbm.1, f32[8]{0:T(128)} %tab_ref.1, s32[1]{0:T(128)} %bitcast.2.cnt_ref, s32[128]{0:T(128)} %bitcast.3, bf16[512,1024]{1,0:T(8,128)(2,1)} %win_hbm.1, ...), custom_call_target="tpu_custom_call" | custom-call | tf_op jit(solution)/shard_map/step/pallas_call | solution.py:950
  76.2 1.0 %place.1 = (f32[16,24,256]{2,1,0:T(8,128)}, f32[64,1024]{1,0:T(8,128)}, f32[128,512]{1,0:T(8,128)}) custom-call(f32[16,24,256]{2,1,0:T(8,128)S(1)} %get-tuple-element.5.final_ref, f32[32,2,2,8,128]{4,3,2,1,0:T(8,128)S(1)} %get-tuple-element.6.sum_ref), custom_call_target="tpu_custom_call" | custom-call | tf_op jit(solution)/shard_map/place/pallas_call | solution.py:984

commit v7 on v6

--- a/solution.py
+++ b/solution.py
@@ -40,14 +40,15 @@
 
 
 def in_order(values, order, parts):
-    total = None
-    rest = values
+    pieces, rest = [], values
     for part in range(parts):
-        piece = rest.astype(BF16)
-        if part < parts - 1:
-            rest = rest - piece.astype(F32)
-        term = matmul(piece, order, ((1,), (0,)))
-        total = term if total is None else total + term
+        pieces.append(rest.astype(BF16))
+        rest = rest - pieces[-1].astype(F32)
+    terms = matmul(jnp.concatenate(pieces, axis=0), order, ((1,), (0,)))
+    rows = values.shape[0]
+    total = terms[0:rows]
+    for part in range(1, parts):
+        total = total + terms[part * rows : (part + 1) * rows]
     return total
 
 
@@ -250,7 +251,7 @@
         return tuple(up), tuple(down)
 
     empty = tuple(jnp.zeros((Y, LANES), F32) for _ in range(3))
-    ups, downs = lax.fori_loop(0, X, pack, (empty, empty))
+    ups, downs = lax.fori_loop(0, X, pack, (empty, empty), unroll=2)
     for i in range(3):
         m.zsend[0, i] = ups[i]
         m.zsend[1, i] = downs[i]
@@ -335,8 +336,8 @@
         return remote(
             m.nsend.at[axis],
             m.nrecv.at[axis, here[axis]],
-            m.n_send.at[axis, step],
-            m.n_recv.at[axis, here[axis]],
+            m.n_send.at[axis],
+            m.n_recv.at[axis],
             line_peer(axis, step),
         )
 
@@ -347,16 +348,12 @@
 
     def count_finish(axis):
         size = sizes[axis]
-        for step in range(1, size):
-            count_copy(axis, step).wait_send()
-            source = lax.rem(here[axis] + step, size)
-            remote(
-                m.nsend.at[axis],
-                m.nrecv.at[axis, source],
-                m.n_send.at[axis, step],
-                m.n_recv.at[axis, source],
-                line_peer(axis, step),
-            ).wait_recv()
+        others = m.nrecv.at[axis, 0 : size - 1]
+        all_of_them = remote(
+            others, others, m.n_send.at[axis], m.n_recv.at[axis], line_peer(axis, 1)
+        )
+        all_of_them.wait_send()
+        all_of_them.wait_recv()
         total = m.nrecv[axis, 0]
         for i in range(1, size):
             total = total + m.nrecv[axis, i]
@@ -689,17 +686,19 @@
         plus, minus, opposed = [lax.rem(me + d, 4) for d in (1, 3, 2)]
         begin, end = pl.ds(0, 2), pl.ds(2, 2)
 
-        def copy(src, dst, number, peer):
-            return remote(src, dst, sems.at[0, number], sems.at[1, number], to(peer))
+        def copy(src, dst, out, into, peer):
+            return remote(src, dst, sems.at[out], sems.at[into], to(peer))
 
         copies = [
-            copy(piece(begin, opposed), relay.at[0], 0, plus),
-            copy(piece(end, opposed), relay.at[1], 1, minus),
-            copy(piece(end, plus), fin.at[0, end], 2, plus),
-            copy(piece(begin, minus), fin.at[1, begin], 3, minus),
-            copy(send.at[0], fin.at[0, begin], 4, plus),
-            copy(send.at[1], fin.at[1, end], 5, minus),
+            copy(piece(begin, opposed), relay.at[0], 0, 2, plus),
+            copy(piece(end, opposed), relay.at[1], 0, 3, minus),
+            copy(piece(end, plus), fin.at[0, end], 1, 4, plus),
+            copy(piece(begin, minus), fin.at[1, begin], 1, 4, minus),
+            copy(send.at[0], fin.at[0, begin], 1, 4, plus),
+            copy(send.at[1], fin.at[1, end], 1, 4, minus),
         ]
+        relays = copy(relay, relay, 0, 2, plus)
+        fins = copy(fin, fin, 1, 4, plus)
 
         def open_ring():
             for one in copies[:4]:
@@ -714,11 +713,10 @@
             copies[5].start()
 
         def close_ring():
-            for one in copies[2:]:
-                one.wait_recv()
+            fins.wait_recv()
             total = piece(pl.ds(0, 4), me)[...] + fin[0] + fin[1]
-            for one in copies:
-                one.wait_send()
+            relays.wait_send()
+            fins.wait_send()
             return total
 
         return open_ring, pass_on, close_ring
@@ -787,8 +785,8 @@
         return remote(
             z_piece(batch, ph, pw),
             m.zgot.at[z_me, batch],
-            m.zp_send.at[batch, number],
-            m.zp_recv.at[batch, z_me],
+            m.zp_send.at[batch],
+            m.zp_recv.at[batch],
             peer,
         )
 
@@ -797,16 +795,11 @@
             z_copy_out(batch, number).start()
         m.zgot[z_me, batch] = z_piece(batch, high, low)[...]
 
-    def z_finish(batch):
-        for number in range(7):
-            ph, pw, slot, peer = z_peers[number]
-            remote(
-                z_piece(batch, high, low),
-                m.zgot.at[slot, batch],
-                m.zp_send.at[batch, number],
-                m.zp_recv.at[batch, slot],
-                peer,
-            ).wait_recv()
+    def z_all(batch):
+        others = m.zgot.at[0:7, batch]
+        return remote(
+            others, others, m.zp_send.at[batch], m.zp_recv.at[batch], z_peers[0][3]
+        )
 
     grad_in = matmul(m.normed[...], m.dpre[...], ((0,), (0,)))
     for h in range(4):
@@ -841,29 +834,32 @@
         return remote(
             m.gathered.at[slot, batch],
             m.gathered.at[slot, batch],
-            m.g_send.at[batch, number],
-            m.g_recv.at[batch, slot],
+            m.g_send.at[batch],
+            m.g_recv.at[batch],
             g_peers[number][1],
         )
 
     for batch in range(2):
-        z_finish(batch)
+        z_all(batch).wait_recv()
         total = m.zgot[0, batch]
         for slot in range(1, 8):
             total = total + m.zgot[slot, batch]
         m.gathered[g_me, batch] = total
         for number in range(31):
             g_copy(batch, number, g_me).start()
+    def g_all(batch):
+        others = m.gathered.at[0:31, batch]
+        return remote(
+            others, others, m.g_send.at[batch], m.g_recv.at[batch], g_peers[0][1]
+        )
+
     for batch in range(2):
-        for number in range(7):
-            z_copy_out(batch, number).wait_send()
+        z_all(batch).wait_send()
     for batch in range(2):
-        for number in range(31):
-            g_copy(batch, number, g_peers[number][0]).wait_recv()
+        g_all(batch).wait_recv()
     sum_ref[...] = m.gathered[...]
     for batch in range(2):
-        for number in range(31):
-            g_copy(batch, number, g_me).wait_send()
+        g_all(batch).wait_send()
 
 
 def step(prev, now, material, table, used, anchors, w_in, w_out, sizes):
@@ -936,16 +932,16 @@
         z_sem=dma((2, 2)),
         f_send=dma((12,)),
         f_recv=dma((2, 12)),
-        n_send=dma((3, most)),
-        n_recv=dma((3, most)),
+        n_send=dma((3,)),
+        n_recv=dma((3,)),
         p_send=dma((2,)),
         p_recv=dma((2,)),
-        sems1=dma((4, 2, 6)),
-        sems2=dma((4, 2, 6)),
-        zp_send=dma((2, 7)),
-        zp_recv=dma((2, 8)),
-        g_send=dma((2, 31)),
-        g_recv=dma((2, 32)),
+        sems1=dma((4, 5)),
+        sems2=dma((4, 5)),
+        zp_send=dma((2,)),
+        zp_recv=dma((2,)),
+        g_send=dma((2,)),
+        g_recv=dma((2,)),
     )
     return pl.pallas_call(
         functools.partial(step_kernel, tuple(scratch), sizes),

time: 77.6 us -> 75.3 us (0.970)
  Pallas kernels: 75.9 us -> 73.4 us
    pallas_call x1, Pallas kernels: 74.9 us -> 72.4 us  [step(): pl.pallas_call(functools.partial(step_kernel, tuple(scratch), sizes), nam...]
where the time goes in v7:
time: 75.3 us; the launch traced here: 74.7 us
  Pallas kernels  73.4 us (97%)
  between operations  1.29 us (2%)
    pallas_call x1, Pallas kernels, step(): pl.pallas_call(functools.partial(step_kernel, tuple(scratch), sizes), nam...  72.4 us

profile of v7, /device:TPU:8, one launch (start us, length us, event | category | flops | bytes accessed | tf_op | source)
XLA Modules:
  0.0 74.7 jit_solution(18393243553798204808)
XLA Ops:
  1.3 72.4 %step.1 = (f32[16,24,256]{2,1,0:T(8,128)S(1)}, f32[32,2,2,8,128]{4,3,2,1,0:T(8,128)S(1)}) custom-call(f32[16,24,256]{2,1,0:T(8,128)} %prev_hbm.1, f32[16,24,256]{2,1,0:T(8,128)} %now_hbm.1, s32[16,24,256]{2,1,0:T(8,128)} %mat_hbm.1, f32[8]{0:T(128)} %tab_ref.1, s32[1]{0:T(128)} %bitcast.2.cnt_ref, s32[128]{0:T(128)} %bitcast.3, bf16[512,1024]{1,0:T(8,128)(2,1)} %win_hbm.1, ...), custom_call_target="tpu_custom_call" | custom-call | tf_op jit(solution)/shard_map/step/pallas_call | solution.py:946
  73.7 1.0 %place.1 = (f32[16,24,256]{2,1,0:T(8,128)}, f32[64,1024]{1,0:T(8,128)}, f32[128,512]{1,0:T(8,128)}) custom-call(f32[16,24,256]{2,1,0:T(8,128)S(1)} %get-tuple-element.5.final_ref, f32[32,2,2,8,128]{4,3,2,1,0:T(8,128)S(1)} %get-tuple-element.6.sum_ref), custom_call_target="tpu_custom_call" | custom-call | tf_op jit(solution)/shard_map/place/pallas_call | solution.py:980

commit v8 on v7

--- a/solution.py
+++ b/solution.py
@@ -174,7 +174,7 @@
     def _():
         m.zrecv[1] = jnp.zeros(m.zrecv.shape[1:], F32)
 
-    for place in reached:
+    for place in reversed(reached):
         signal(barrier, place)
 
     lane = lax.broadcasted_iota(jnp.int32, (Y, LANES), 1)
@@ -439,12 +439,12 @@
                     half, tile * LANES : (tile + 1) * LANES, :
                 ].T
 
-    def pick_one(s, first_row, keep):
+    def pick_one(s, first_row, by):
         first = m.turned[pl.ds(first_row, 8), :]
         second = m.turned[pl.ds(first_row + Z, 8), :]
-        back = jnp.bitwise_and(keep, LANES - 1)
-        m.picked[pl.ds(pl.multiple_of(s * 8, 8), 8), :] = jnp.where(
-            narrow < keep, pltpu.roll(first, back, 1), pltpu.roll(second, back, 1)
+        back = jnp.bitwise_and(LANES - by, LANES - 1)
+        m.picked[pl.ds(pl.multiple_of(s * 8, 8), 8), :] = pltpu.roll(
+            jnp.where(narrow >= by, first, second), back, 1
         )
 
     def pick_inputs(s, carry):
@@ -454,10 +454,10 @@
         j = rest // Z
         shift = j * X + i
         first_row = (shift // LANES) * Z + (rest - j * Z)
-        keep = LANES - jnp.bitwise_and(shift, LANES - 1)
+        by = jnp.bitwise_and(shift, LANES - 1)
         m.where[0, s] = first_row
-        m.where[1, s] = keep
-        pick_one(s, first_row, keep)
+        m.where[1, s] = by
+        pick_one(s, first_row, by)
         return carry
 
     def pick_targets(s, carry):
@@ -574,7 +574,6 @@
             came(range(4), 0, 2)
         else:
             came(range(4), par, 0)
-        came(range(4, 8), par, 0)
         for side in range(2):
             for e in range(2):
                 plane = e + side * (X + 2)
@@ -582,11 +581,6 @@
                     A[rows_of(plane, t), :] = value
             for t, value in enumerate(face_tiles(m.yrecv, (par, side), 0)):
                 A[rows_over(t, -1 if side == 0 else Y), :] = value
-        for t in range(T):
-            for i in range(4):
-                plane = 1 if i < 2 else X + 2
-                at = -1 if i % 2 == 0 else Y
-                A[rows_of(plane, t, at, 1), :] = m.crecv[par, i, :, tile_of(t)]
         if r == 0:
             for side, plane, ring_coef in ((0, 1, 0), (1, X + 2, X + 1)):
                 olds = face_tiles(m.xrecv, (0, side), 2)
@@ -600,14 +594,22 @@
                     m.yold[side, t] = side_olds[t]
                     m.ycoef[side, t] = side_coefs[t]
 
-        for p in (1, 2, X + 1, X + 2):
-            first(p)
+        first(2)
+        first(X + 1)
         for side in range(2):
             at = side * (Y - 1)
             old = whole([m.held_rows[side, t] for t in range(T)])
             value = row_update(A, old, at)
             for t in range(T):
                 B[rows_over(t, at), :] = value[:, tile_of(t)]
+        came(range(4, 8), par, 0)
+        for t in range(T):
+            for i in range(4):
+                plane = 1 if i < 2 else X + 2
+                at = -1 if i % 2 == 0 else Y
+                A[rows_of(plane, t, at, 1), :] = m.crecv[par, i, :, tile_of(t)]
+        first(1)
+        first(X + 2)
         for side in range(2):
 
             def plane_of(ref, *index):
@@ -646,13 +648,14 @@
                 for at in rows:
                     old = whole([A[rows_over(t, at), :] for t in range(T)])
                     values.append(row_update(B, old, at))
+                m.csend[side] = values[0][0:1]
+                m.csend[2 + side] = values[0][X - 1 : X]
+                start((4 + side, 6 + side), 1 - par, 0)
                 sources = [lambda t, v=v: v[:, tile_of(t)] for v in values]
                 put_face(m.ysend, side, sources, True, True)
                 start((2 + side,), 1 - par, 0)
             for p in (2, 3, X, X + 1):
                 second(p)
-            put_lines()
-            start(range(4, 8), 1 - par, 0)
             put_planes(2, True, True)
             start(range(2), 1 - par, 0)
             lax.fori_loop(4, X, second, 0, unroll=2)

time: 75.3 us -> 74.2 us (0.985)
  Pallas kernels: 73.4 us -> 72.5 us
    pallas_call x1, Pallas kernels: 72.4 us -> 71.5 us  [step(): pl.pallas_call(functools.partial(step_kernel, tuple(scratch), sizes), nam...]
where the time goes in v8:
time: 74.2 us; the launch traced here: 73.8 us
  Pallas kernels  72.5 us (98%)
  between operations  1.29 us (2%)
    pallas_call x1, Pallas kernels, step(): pl.pallas_call(functools.partial(step_kernel, tuple(scratch), sizes), nam...  71.5 us

profile of v8, /device:TPU:8, one launch (start us, length us, event | category | flops | bytes accessed | tf_op | source)
XLA Modules:
  0.0 73.8 jit_solution(4892679656302410370)
XLA Ops:
  1.3 71.5 %step.1 = (f32[16,24,256]{2,1,0:T(8,128)S(1)}, f32[32,2,2,8,128]{4,3,2,1,0:T(8,128)S(1)}) custom-call(f32[16,24,256]{2,1,0:T(8,128)} %prev_hbm.1, f32[16,24,256]{2,1,0:T(8,128)} %now_hbm.1, s32[16,24,256]{2,1,0:T(8,128)} %mat_hbm.1, f32[8]{0:T(128)} %tab_ref.1, s32[1]{0:T(128)} %bitcast.2.cnt_ref, s32[128]{0:T(128)} %bitcast.3, bf16[512,1024]{1,0:T(8,128)(2,1)} %win_hbm.1, ...), custom_call_target="tpu_custom_call" | custom-call | tf_op jit(solution)/shard_map/step/pallas_call | solution.py:949
  72.8 1.0 %place.1 = (f32[16,24,256]{2,1,0:T(8,128)}, f32[64,1024]{1,0:T(8,128)}, f32[128,512]{1,0:T(8,128)}) custom-call(f32[16,24,256]{2,1,0:T(8,128)S(1)} %get-tuple-element.5.final_ref, f32[32,2,2,8,128]{4,3,2,1,0:T(8,128)S(1)} %get-tuple-element.6.sum_ref), custom_call_target="tpu_custom_call" | custom-call | tf_op jit(solution)/shard_map/place/pallas_call | solution.py:983

commit v9 on v8

--- a/solution.py
+++ b/solution.py
@@ -117,6 +117,8 @@
     g_steps = [
         (i, j, l) for i in range(4) for j in range(4) for l in range(2) if i or j or l
     ]
+    z_steps.sort(key=lambda p: -(2 * min(p[0], 4 - p[0]) + p[1]))
+    g_steps.sort(key=lambda p: -(min(p[0], 4 - p[0]) + min(p[1], 4 - p[1]) + p[2]))
     reached = []
     for axis in range(3):
         for step in range(1, sizes[axis]):
@@ -860,7 +862,7 @@
         z_all(batch).wait_send()
     for batch in range(2):
         g_all(batch).wait_recv()
-    sum_ref[...] = m.gathered[...]
+        sum_ref[:, batch] = m.gathered[:, batch]
     for batch in range(2):
         g_all(batch).wait_send()
 

time: 74.2 us -> 72.9 us (0.982)
  Pallas kernels: 72.5 us -> 71.2 us
    pallas_call x1, Pallas kernels: 71.5 us -> 70.2 us  [step(): pl.pallas_call(functools.partial(step_kernel, tuple(scratch), sizes), nam...]
where the time goes in v9:
time: 72.9 us; the launch traced here: 72.4 us
  Pallas kernels  71.2 us (98%)
  between operations  1.29 us (2%)
    pallas_call x1, Pallas kernels, step(): pl.pallas_call(functools.partial(step_kernel, tuple(scratch), sizes), nam...  70.2 us

profile of v9, /device:TPU:8, one launch (start us, length us, event | category | flops | bytes accessed | tf_op | source)
XLA Modules:
  0.0 72.4 jit_solution(6829665881798815842)
XLA Ops:
  1.3 70.2 %step.1 = (f32[16,24,256]{2,1,0:T(8,128)S(1)}, f32[32,2,2,8,128]{4,3,2,1,0:T(8,128)S(1)}) custom-call(f32[16,24,256]{2,1,0:T(8,128)} %prev_hbm.1, f32[16,24,256]{2,1,0:T(8,128)} %now_hbm.1, s32[16,24,256]{2,1,0:T(8,128)} %mat_hbm.1, f32[8]{0:T(128)} %tab_ref.1, s32[1]{0:T(128)} %bitcast.2.cnt_ref, s32[128]{0:T(128)} %bitcast.3, bf16[512,1024]{1,0:T(8,128)(2,1)} %win_hbm.1, ...), custom_call_target="tpu_custom_call" | custom-call | tf_op jit(solution)/shard_map/step/pallas_call | solution.py:951
  71.5 1.0 %place.1 = (f32[16,24,256]{2,1,0:T(8,128)}, f32[64,1024]{1,0:T(8,128)}, f32[128,512]{1,0:T(8,128)}) custom-call(f32[16,24,256]{2,1,0:T(8,128)S(1)} %get-tuple-element.5.final_ref, f32[32,2,2,8,128]{4,3,2,1,0:T(8,128)S(1)} %get-tuple-element.6.sum_ref), custom_call_target="tpu_custom_call" | custom-call | tf_op jit(solution)/shard_map/place/pallas_call | solution.py:985
